TPU v7x, 256 devices: a whole 4x4x8 slice. The times are simulated.
256 devices in a mesh: seq: 16 (over x, y), mp: 16 (over z, core).
Axes of the slice: x: 4, y: 4, z: 8, core: 2. Of those that a mesh axis runs over, the one named last changes fastest.
Arguments:
- features: bfloat16 [32768, 16384], P('seq', 'mp'), may hold values from -6 to 6
- coupling: bfloat16 [32768, 256], P('seq'), may hold values from -6 to 6
- gate_values: bfloat16 [32768, 16384], P('seq', 'mp'), may hold values from -40 to 40
- step_raw: float32 [256, 32768], P('mp', 'seq'), may hold values from -12 to 32768
- decay_log: float32 [256], P('mp'), may hold values from -8 to 0
- feature_taps: float32 [4, 16384], P(None, 'mp'), may hold values from -3 to 3
- feature_offset: float32 [16384], P('mp'), may hold values from -3 to 3
- coupling_taps: float32 [4, 256], replicated, may hold values from -3 to 3
- coupling_offset: float32 [256], replicated, may hold values from -3 to 3
- norm_gain: float32 [16384], P('mp'), may hold values from 0.25 to 1.75
Outputs:
- normalized: bfloat16 [32768, 16384], P('seq', 'mp')
All inputs are finite; a program needn't handle non-finite values.
Results may differ from a plain program's by a relative error of at most 0.0061.
Values may be sent and summed in bfloat16 or wider, within the bound.
No kernel may reach another device: no remote copies, remote signals or barrier semaphores. Data moves between devices by JAX's collectives and lax.ppermute only.
A program may use at most 128 MiB of HBM per device.

v0:
```python
import jax
import jax.numpy as jnp
from jax import lax
from jax.sharding import PartitionSpec as P

BLOCK = 256
INNER = 16384


FULL_PRECISION = lax.Precision.HIGHEST


def passed_along(block, axis, distance):
    devices = range(lax.axis_size(axis))
    route = [(i - distance, i) for i in devices if i - distance in devices]
    return lax.ppermute(block, axis, route)


def causal_mix(previous, current, weight, bias_row):
    tap_count = weight.shape[0]
    length = current.shape[0]
    padded = jnp.concatenate([previous, current], axis=0)
    running = jnp.zeros(current.shape, jnp.float32) + bias_row[None, :]
    for offset in range(tap_count):
        running = running + weight[offset][None, :] * padded[offset : offset + length].astype(
            jnp.float32
        )
    return jax.nn.silu(running).astype(jnp.bfloat16)


def block_pass(state_now, inputs):
    feature_block, input_map, output_map, step_block, log_block = inputs
    head_count, block_len = step_block.shape
    feature = feature_block.shape[1] // head_count
    per_head = feature_block.astype(jnp.float32).reshape(block_len, head_count, feature)
    scores = jnp.dot(output_map, input_map.T, precision=FULL_PRECISION)
    spread = log_block[:, :, None] - log_block[:, None, :]
    causal = (jnp.arange(block_len)[:, None] >= jnp.arange(block_len)[None, :])[None, :, :]
    weights = jnp.where(causal, jnp.exp(jnp.where(causal, spread, 0.0)), 0.0)
    weights = weights * scores[None, :, :] * step_block[:, None, :]
    inside = jnp.einsum("hts,shp->thp", weights, per_head, precision=FULL_PRECISION)
    carried = jnp.einsum("tn,hpn->thp", output_map, state_now, precision=FULL_PRECISION)
    carried = carried * jnp.exp(log_block).T[:, :, None]
    ending = log_block[:, -1]
    to_end = jnp.exp(ending[:, None] - log_block) * step_block
    weighted = per_head * to_end.T[:, :, None]
    fresh_part = jnp.einsum("shp,sn->hpn", weighted, input_map, precision=FULL_PRECISION)
    new_state = jnp.exp(ending)[:, None, None] * state_now + fresh_part
    return (new_state, (inside + carried).reshape(block_len, head_count * feature))


def on_device(
    features,
    coupling,
    gate_values,
    step_raw,
    decay_log,
    feature_taps,
    feature_offset,
    coupling_taps,
    coupling_offset,
    norm_gain,
):
    tok_count = features.shape[0]
    tap_count = feature_taps.shape[0]
    head_count = decay_log.shape[0]
    state_size = coupling.shape[1] // 2
    feature = features.shape[1] // head_count
    tail_start = tok_count - tap_count + 1
    prior_features, prior_coupling = passed_along(
        (features[tail_start:], coupling[tail_start:]), "seq", 1
    )
    filtered = causal_mix(prior_features, features, feature_taps, feature_offset)
    coupled = causal_mix(prior_coupling, coupling, coupling_taps, coupling_offset).astype(
        jnp.float32
    )
    input_map = coupled[:, :state_size]
    output_map = coupled[:, state_size:]
    increment_amount = jax.nn.softplus(step_raw)
    log_decay = -jnp.exp(decay_log)[:, None] * increment_amount
    blocks = tok_count // BLOCK
    log_inside = jnp.cumsum(log_decay.reshape(head_count, blocks, BLOCK), axis=2)
    inputs = (
        filtered.reshape(blocks, BLOCK, head_count * feature),
        input_map.reshape(blocks, BLOCK, state_size),
        output_map.reshape(blocks, BLOCK, state_size),
        increment_amount.reshape(head_count, blocks, BLOCK).transpose(1, 0, 2),
        log_inside.transpose(1, 0, 2),
    )
    zero_state = jnp.zeros((head_count, feature, state_size), jnp.float32)
    local_end, local_out = lax.scan(block_pass, zero_state, inputs)
    local_out = local_out.reshape(tok_count, head_count * feature)
    section_decay = jnp.exp(jnp.sum(log_decay, axis=1))

    def relay_step(turn_index, incoming):
        return passed_along(section_decay[:, None, None] * incoming + local_end, "seq", 1)

    entering = lax.fori_loop(0, lax.axis_size("seq") - 1, relay_step, jnp.zeros_like(local_end))
    log_running = jnp.cumsum(log_decay, axis=1)
    from_before = jnp.einsum("tn,hpn->thp", output_map, entering, precision=FULL_PRECISION)
    from_before = from_before * jnp.exp(log_running).T[:, :, None]
    scan_values = local_out + from_before.reshape(tok_count, head_count * feature)
    gated_values = scan_values * jax.nn.silu(gate_values.astype(jnp.float32))
    squares = lax.psum(jnp.sum(gated_values * gated_values, axis=1), "mp")
    mean_square = squares / INNER
    return (gated_values * norm_gain[None, :] * lax.rsqrt(mean_square + 1e-05)[:, None]).astype(
        jnp.bfloat16
    )


def solution(mesh):
    in_specs = (
        P("seq", "mp"),
        P("seq", None),
        P("seq", "mp"),
        P("mp", "seq"),
        P("mp"),
        P(None, "mp"),
        P("mp"),
        P(),
        P(),
        P("mp"),
    )
    out_specs = P("seq", "mp")
    return jax.shard_map(
        on_device, mesh=mesh, in_specs=in_specs, out_specs=out_specs, check_vma=False
    )
```

profile of v0, /device:TPU:7, one launch (start us, length us, event | category | flops | bytes accessed | tf_op | source)
XLA Modules:
  0.0 438.5 jit_solution(13467338180037650684)
XLA Ops:
  15.8 9.0 %reduce-window.14 = f32[16,8,2,128]{3,1,2,0:T(8,128)S(1)} reduce-window(f32[16,8,2,128]{3,1,2,0:T(8,128)S(1)} %copy.26, f32[]{:T(128)} %constant.42.clone.1), window={size=1x1x1x128 pad=0_0x0_0x0_0x127_0}, to_apply=%region_0.1 | reduce-window | flops 4161536 | bytes 262148 | tf_op jit(solution)/shard_map/reduce-window
  31.7 6.9 %multiply_convert_fusion.1 = bf16[2048,1024]{1,0:T(8,128)(2,1)} fusion(bf16[2048,1024]{1,0:T(8,128)(2,1)S(1)} %copy-done.2, bf16[3,1024]{1,0:T(4,128)(2,1)S(1)} %collective-permute-done.1, f32[1024]{0:T(1024)S(1)} %bitcast.128, f32[1024]{0:T(1024)S(1)} %bitcast.129, f32[1024]{0:T(1024)S(1)} %bitcast.127, f32[1024]{0:T(1024)S(1)} %bitcast.126, ...), kind=kLoop, calls=%fused_computation.55 | loop fusion | flops 54525952 | bytes 8415232 | tf_op jit(solution)/shard_map/convert_element_type | solution.py:28
  38.6 102.9 %while.24 = (s32[]{:T(128)}, f32[16,64,128]{2,1,0:T(8,128)S(1)}, f32[8,256,1024]{2,1,0:T(8,128)}, f32[8,16,256]{2,0,1:T(8,128)S(1)}, bf16[8,256,1024]{2,1,0:T(8,...) while((s32[]{:T(128)}, f32[16,64,128]{2,1,0:T(8,128)S(1)}, ...), condition=%wide.region_3.4_spmd.clone, body=%wide.region_2.3_spmd.clone.sunk | while | flops 1718165504 | bytes 15681040 | solution.py:91
  141.6 222.4 %while.23 = (s32[]{:T(128)}, f32[16,64,128]{2,1,0:T(8,128)S(1)}, f32[16]{0:T(128)S(1)}, f32[16,64,128]{2,1,0:T(8,128)S(1)}, s32[]{:T(128)}) while((s32[]{:T(128)}, f32[16,64,128]{2,1,0:T(8,128)S(1)}, f32[16]{0:T(128)S(1)}, f32[16,64,128]{2,1,0:T(8,128)S(1)}, s32[]{:T(128)}) %tuple.54), condition=%wide.region_6.7_spmd, body=%wide.region_5.6_spmd.sunk | while | flops 262146 | bytes 3670181 | solution.py:98
  144.7 13.3 %collective-permute-done = f32[16,64,128]{2,1,0:T(8,128)S(1)} collective-permute-done((f32[16,64,128]{2,1,0:T(8,128)S(1)}, f32[16,64,128]{2,1,0:T(8,128)S(1)}, u32[]{:S(2)}, u32[]{:S(2)}) %collective-permute-start) | collective-permute-done | bytes 524320 | tf_op jit(solution)/shard_map/while/body/eval_jaxpr/ppermute | solution.py:16
  160.1 13.5 %collective-permute-done = f32[16,64,128]{2,1,0:T(8,128)S(1)} collective-permute-done((f32[16,64,128]{2,1,0:T(8,128)S(1)}, f32[16,64,128]{2,1,0:T(8,128)S(1)}, u32[]{:S(2)}, u32[]{:S(2)}) %collective-permute-start) | collective-permute-done | bytes 524320 | tf_op jit(solution)/shard_map/while/body/eval_jaxpr/ppermute | solution.py:16
  175.6 12.6 %collective-permute-done = f32[16,64,128]{2,1,0:T(8,128)S(1)} collective-permute-done((f32[16,64,128]{2,1,0:T(8,128)S(1)}, f32[16,64,128]{2,1,0:T(8,128)S(1)}, u32[]{:S(2)}, u32[]{:S(2)}) %collective-permute-start) | collective-permute-done | bytes 524320 | tf_op jit(solution)/shard_map/while/body/eval_jaxpr/ppermute | solution.py:16
  190.3 11.7 %collective-permute-done = f32[16,64,128]{2,1,0:T(8,128)S(1)} collective-permute-done((f32[16,64,128]{2,1,0:T(8,128)S(1)}, f32[16,64,128]{2,1,0:T(8,128)S(1)}, u32[]{:S(2)}, u32[]{:S(2)}) %collective-permute-start) | collective-permute-done | bytes 524320 | tf_op jit(solution)/shard_map/while/body/eval_jaxpr/ppermute | solution.py:16
  204.1 10.9 %collective-permute-done = f32[16,64,128]{2,1,0:T(8,128)S(1)} collective-permute-done((f32[16,64,128]{2,1,0:T(8,128)S(1)}, f32[16,64,128]{2,1,0:T(8,128)S(1)}, u32[]{:S(2)}, u32[]{:S(2)}) %collective-permute-start) | collective-permute-done | bytes 524320 | tf_op jit(solution)/shard_map/while/body/eval_jaxpr/ppermute | solution.py:16
  217.0 10.1 %collective-permute-done = f32[16,64,128]{2,1,0:T(8,128)S(1)} collective-permute-done((f32[16,64,128]{2,1,0:T(8,128)S(1)}, f32[16,64,128]{2,1,0:T(8,128)S(1)}, u32[]{:S(2)}, u32[]{:S(2)}) %collective-permute-start) | collective-permute-done | bytes 524320 | tf_op jit(solution)/shard_map/while/body/eval_jaxpr/ppermute | solution.py:16
  229.2 10.1 %collective-permute-done = f32[16,64,128]{2,1,0:T(8,128)S(1)} collective-permute-done((f32[16,64,128]{2,1,0:T(8,128)S(1)}, f32[16,64,128]{2,1,0:T(8,128)S(1)}, u32[]{:S(2)}, u32[]{:S(2)}) %collective-permute-start) | collective-permute-done | bytes 524320 | tf_op jit(solution)/shard_map/while/body/eval_jaxpr/ppermute | solution.py:16
  241.3 10.7 %collective-permute-done = f32[16,64,128]{2,1,0:T(8,128)S(1)} collective-permute-done((f32[16,64,128]{2,1,0:T(8,128)S(1)}, f32[16,64,128]{2,1,0:T(8,128)S(1)}, u32[]{:S(2)}, u32[]{:S(2)}) %collective-permute-start) | collective-permute-done | bytes 524320 | tf_op jit(solution)/shard_map/while/body/eval_jaxpr/ppermute | solution.py:16
  254.1 11.8 %collective-permute-done = f32[16,64,128]{2,1,0:T(8,128)S(1)} collective-permute-done((f32[16,64,128]{2,1,0:T(8,128)S(1)}, f32[16,64,128]{2,1,0:T(8,128)S(1)}, u32[]{:S(2)}, u32[]{:S(2)}) %collective-permute-start) | collective-permute-done | bytes 524320 | tf_op jit(solution)/shard_map/while/body/eval_jaxpr/ppermute | solution.py:16
  268.0 13.0 %collective-permute-done = f32[16,64,128]{2,1,0:T(8,128)S(1)} collective-permute-done((f32[16,64,128]{2,1,0:T(8,128)S(1)}, f32[16,64,128]{2,1,0:T(8,128)S(1)}, u32[]{:S(2)}, u32[]{:S(2)}) %collective-permute-start) | collective-permute-done | bytes 524320 | tf_op jit(solution)/shard_map/while/body/eval_jaxpr/ppermute | solution.py:16
  283.0 14.1 %collective-permute-done = f32[16,64,128]{2,1,0:T(8,128)S(1)} collective-permute-done((f32[16,64,128]{2,1,0:T(8,128)S(1)}, f32[16,64,128]{2,1,0:T(8,128)S(1)}, u32[]{:S(2)}, u32[]{:S(2)}) %collective-permute-start) | collective-permute-done | bytes 524320 | tf_op jit(solution)/shard_map/while/body/eval_jaxpr/ppermute | solution.py:16
  299.2 15.3 %collective-permute-done = f32[16,64,128]{2,1,0:T(8,128)S(1)} collective-permute-done((f32[16,64,128]{2,1,0:T(8,128)S(1)}, f32[16,64,128]{2,1,0:T(8,128)S(1)}, u32[]{:S(2)}, u32[]{:S(2)}) %collective-permute-start) | collective-permute-done | bytes 524320 | tf_op jit(solution)/shard_map/while/body/eval_jaxpr/ppermute | solution.py:16
  316.5 15.3 %collective-permute-done = f32[16,64,128]{2,1,0:T(8,128)S(1)} collective-permute-done((f32[16,64,128]{2,1,0:T(8,128)S(1)}, f32[16,64,128]{2,1,0:T(8,128)S(1)}, u32[]{:S(2)}, u32[]{:S(2)}) %collective-permute-start) | collective-permute-done | bytes 524320 | tf_op jit(solution)/shard_map/while/body/eval_jaxpr/ppermute | solution.py:16
  333.9 14.5 %collective-permute-done = f32[16,64,128]{2,1,0:T(8,128)S(1)} collective-permute-done((f32[16,64,128]{2,1,0:T(8,128)S(1)}, f32[16,64,128]{2,1,0:T(8,128)S(1)}, u32[]{:S(2)}, u32[]{:S(2)}) %collective-permute-start) | collective-permute-done | bytes 524320 | tf_op jit(solution)/shard_map/while/body/eval_jaxpr/ppermute | solution.py:16
  350.4 13.6 %collective-permute-done = f32[16,64,128]{2,1,0:T(8,128)S(1)} collective-permute-done((f32[16,64,128]{2,1,0:T(8,128)S(1)}, f32[16,64,128]{2,1,0:T(8,128)S(1)}, u32[]{:S(2)}, u32[]{:S(2)}) %collective-permute-start) | collective-permute-done | bytes 524320 | tf_op jit(solution)/shard_map/while/body/eval_jaxpr/ppermute | solution.py:16
  364.0 5.6 %convolution_multiply_fusion.1 = f32[2048,16,64]{0,2,1:T(8,128)} fusion(f32[16,64,128]{2,1,0:T(8,128)S(1)} %get-tuple-element.72, f32[2048,16]{0,1:T(8,128)S(1)} %bitcast.121, bf16[2048,256]{1,0:T(8,128)(2,1)S(1)} %copy-done.1), kind=kOutput, calls=%fused_computation.58 | convolution fusion | flops 3223322624 | bytes 9568256 | tf_op jit(solution)/shard_map/tn,hpn->thp/dot_general | solution.py:100
  369.6 9.3 %copy.33 = f32[2048,1024]{1,0:T(8,128)} copy(f32[2048,1024]{0,1:T(8,128)} %bitcast.116) | data formatting | bytes 16777216 | tf_op jit(solution)/shard_map/reshape | solution.py:102
  378.8 11.9 %multiply_reduce_fusion = (f32[2048]{0:T(1024)S(1)}, f32[2048,1024]{1,0:T(8,128)}) fusion(bf16[2048,1024]{1,0:T(8,128)(2,1)} %param.16, f32[2048,1024]{1,0:T(8,128)} %copy.33, f32[8,256,1024]{2,1,0:T(8,128)} %get-tuple-element.70), kind=kLoop, calls=%fused_computation.54 | loop fusion | flops 18872320 | bytes 29368320 | tf_op jit(solution)/shard_map/reduce_sum | solution.py:104
  390.7 42.5 %psum.7 = f32[2048]{0:T(1024)S(1)} all-reduce(f32[2048]{0:T(1024)S(1)} %get-tuple-element.142), channel_id=1, replica_groups=mesh['seq'=16,'mp'=16] {'mp'}, use_global_device_ids=true, to_apply=%region_10.11 | all-reduce | flops 2048 | bytes 16384 | tf_op jit(solution)/shard_map/psum | solution.py:104
  433.3 5.2 %multiply_convert_fusion = bf16[2048,1024]{1,0:T(8,128)(2,1)} fusion(f32[2048,1024]{1,0:T(8,128)} %get-tuple-element.143, f32[2048]{0:T(1024)S(1)} %add_rsqrt_fusion, f32[1024]{0:T(1024)S(1)} %copy-done.4), kind=kLoop, calls=%fused_computation.53 | loop fusion | flops 6291456 | bytes 12595200 | tf_op jit(solution)/shard_map/convert_element_type | solution.py:106
  (228 shorter events, 156.5 us)
Async XLA Ops:
  0.0 27.6 %copy-start.3 = (bf16[2048,256]{1,0:T(8,128)(2,1)S(1)}, bf16[2048,256]{1,0:T(8,128)(2,1)}, u32[]{:S(2)}) copy-start(bf16[2048,256]{1,0:T(8,128)(2,1)} %param.15) | copy-start | bytes 3145732
  0.0 27.6 %copy-start.6 = (f32[256]{0:T(256)S(1)}, f32[256]{0:T(256)}, u32[]{:S(2)}) copy-start(f32[256]{0:T(256)} %param.22) | copy-start | bytes 3076
  0.8 26.8 %collective-permute-start.2 = (bf16[3,256]{1,0:T(4,128)(2,1)S(1)}, bf16[3,256]{1,0:T(4,128)(2,1)S(1)}, u32[]{:S(2)}, u32[]{:S(2)}) collective-permute-start(bf16[3,256]{1,0:T(4,128)(2,1)S(1)} %slice.82), channel_id=1, source_target_pairs={{0,16},{16,32},{32,48},{48,64},{64,80},{80,96},{96,112},{112,128},... | collective-permute-start | bytes 4616 | tf_op jit(solution)/shard_map/ppermute | solution.py:16
  4.7 26.9 %collective-permute-start.1 = (bf16[3,1024]{1,0:T(4,128)(2,1)S(1)}, bf16[3,1024]{1,0:T(4,128)(2,1)S(1)}, u32[]{:S(2)}, u32[]{:S(2)}) collective-permute-start(bf16[3,1024]{1,0:T(4,128)(2,1)S(1)} %slice.74), channel_id=1, source_target_pairs={{0,16},{16,32},{32,48},{48,64},{64,80},{80,96},{96,112},{112,128},... | collective-permute-start | bytes 18440 | tf_op jit(solution)/shard_map/ppermute | solution.py:16
  24.8 6.8 %copy-start.5 = (f32[1024]{0:T(1024)S(1)}, f32[1024]{0:T(1024)}, u32[]{:S(2)}) copy-start(f32[1024]{0:T(1024)} %param.20) | copy-start | bytes 12292
  27.6 4.1 copy-start.2
  29.1 1.1 copy-start
  141.5 222.5 %copy-start.1 = (bf16[2048,256]{1,0:T(8,128)(2,1)S(1)}, bf16[2048,256]{1,0:T(8,128)(2,1)}, u32[]{:S(2)}) copy-start(bf16[2048,256]{1,0:T(8,128)(2,1)} %copy-done) | copy-start | bytes 3145732
  141.7 16.4 %collective-permute-start = (f32[16,64,128]{2,1,0:T(8,128)S(1)}, f32[16,64,128]{2,1,0:T(8,128)S(1)}, u32[]{:S(2)}, u32[]{:S(2)}) collective-permute-start(f32[16,64,128]{2,1,0:T(8,128)S(1)} %multiply_add_fusion.2), channel_id=1, source_target_pairs={{0,16},{16,32},{32,48},{48,64},{64,80},{80,96},{96,112},{112,128},... | collective-permute-start | bytes 1572872 | tf_op jit(solution)/shard_map/while/body/eval_jaxpr/ppermute | solution.py:16
  158.2 15.4 %collective-permute-start = (f32[16,64,128]{2,1,0:T(8,128)S(1)}, f32[16,64,128]{2,1,0:T(8,128)S(1)}, u32[]{:S(2)}, u32[]{:S(2)}) collective-permute-start(f32[16,64,128]{2,1,0:T(8,128)S(1)} %multiply_add_fusion.2), channel_id=1, source_target_pairs={{0,16},{16,32},{32,48},{48,64},{64,80},{80,96},{96,112},{112,128},... | collective-permute-start | bytes 1572872 | tf_op jit(solution)/shard_map/while/body/eval_jaxpr/ppermute | solution.py:16
  173.7 14.5 %collective-permute-start = (f32[16,64,128]{2,1,0:T(8,128)S(1)}, f32[16,64,128]{2,1,0:T(8,128)S(1)}, u32[]{:S(2)}, u32[]{:S(2)}) collective-permute-start(f32[16,64,128]{2,1,0:T(8,128)S(1)} %multiply_add_fusion.2), channel_id=1, source_target_pairs={{0,16},{16,32},{32,48},{48,64},{64,80},{80,96},{96,112},{112,128},... | collective-permute-start | bytes 1572872 | tf_op jit(solution)/shard_map/while/body/eval_jaxpr/ppermute | solution.py:16
  188.4 13.7 %collective-permute-start = (f32[16,64,128]{2,1,0:T(8,128)S(1)}, f32[16,64,128]{2,1,0:T(8,128)S(1)}, u32[]{:S(2)}, u32[]{:S(2)}) collective-permute-start(f32[16,64,128]{2,1,0:T(8,128)S(1)} %multiply_add_fusion.2), channel_id=1, source_target_pairs={{0,16},{16,32},{32,48},{48,64},{64,80},{80,96},{96,112},{112,128},... | collective-permute-start | bytes 1572872 | tf_op jit(solution)/shard_map/while/body/eval_jaxpr/ppermute | solution.py:16
  202.2 12.8 %collective-permute-start = (f32[16,64,128]{2,1,0:T(8,128)S(1)}, f32[16,64,128]{2,1,0:T(8,128)S(1)}, u32[]{:S(2)}, u32[]{:S(2)}) collective-permute-start(f32[16,64,128]{2,1,0:T(8,128)S(1)} %multiply_add_fusion.2), channel_id=1, source_target_pairs={{0,16},{16,32},{32,48},{48,64},{64,80},{80,96},{96,112},{112,128},... | collective-permute-start | bytes 1572872 | tf_op jit(solution)/shard_map/while/body/eval_jaxpr/ppermute | solution.py:16
  215.1 12.0 %collective-permute-start = (f32[16,64,128]{2,1,0:T(8,128)S(1)}, f32[16,64,128]{2,1,0:T(8,128)S(1)}, u32[]{:S(2)}, u32[]{:S(2)}) collective-permute-start(f32[16,64,128]{2,1,0:T(8,128)S(1)} %multiply_add_fusion.2), channel_id=1, source_target_pairs={{0,16},{16,32},{32,48},{48,64},{64,80},{80,96},{96,112},{112,128},... | collective-permute-start | bytes 1572872 | tf_op jit(solution)/shard_map/while/body/eval_jaxpr/ppermute | solution.py:16
  227.3 12.0 %collective-permute-start = (f32[16,64,128]{2,1,0:T(8,128)S(1)}, f32[16,64,128]{2,1,0:T(8,128)S(1)}, u32[]{:S(2)}, u32[]{:S(2)}) collective-permute-start(f32[16,64,128]{2,1,0:T(8,128)S(1)} %multiply_add_fusion.2), channel_id=1, source_target_pairs={{0,16},{16,32},{32,48},{48,64},{64,80},{80,96},{96,112},{112,128},... | collective-permute-start | bytes 1572872 | tf_op jit(solution)/shard_map/while/body/eval_jaxpr/ppermute | solution.py:16
  239.4 12.6 %collective-permute-start = (f32[16,64,128]{2,1,0:T(8,128)S(1)}, f32[16,64,128]{2,1,0:T(8,128)S(1)}, u32[]{:S(2)}, u32[]{:S(2)}) collective-permute-start(f32[16,64,128]{2,1,0:T(8,128)S(1)} %multiply_add_fusion.2), channel_id=1, source_target_pairs={{0,16},{16,32},{32,48},{48,64},{64,80},{80,96},{96,112},{112,128},... | collective-permute-start | bytes 1572872 | tf_op jit(solution)/shard_map/while/body/eval_jaxpr/ppermute | solution.py:16
  252.2 13.8 %collective-permute-start = (f32[16,64,128]{2,1,0:T(8,128)S(1)}, f32[16,64,128]{2,1,0:T(8,128)S(1)}, u32[]{:S(2)}, u32[]{:S(2)}) collective-permute-start(f32[16,64,128]{2,1,0:T(8,128)S(1)} %multiply_add_fusion.2), channel_id=1, source_target_pairs={{0,16},{16,32},{32,48},{48,64},{64,80},{80,96},{96,112},{112,128},... | collective-permute-start | bytes 1572872 | tf_op jit(solution)/shard_map/while/body/eval_jaxpr/ppermute | solution.py:16
  266.0 14.9 %collective-permute-start = (f32[16,64,128]{2,1,0:T(8,128)S(1)}, f32[16,64,128]{2,1,0:T(8,128)S(1)}, u32[]{:S(2)}, u32[]{:S(2)}) collective-permute-start(f32[16,64,128]{2,1,0:T(8,128)S(1)} %multiply_add_fusion.2), channel_id=1, source_target_pairs={{0,16},{16,32},{32,48},{48,64},{64,80},{80,96},{96,112},{112,128},... | collective-permute-start | bytes 1572872 | tf_op jit(solution)/shard_map/while/body/eval_jaxpr/ppermute | solution.py:16
  281.1 16.1 %collective-permute-start = (f32[16,64,128]{2,1,0:T(8,128)S(1)}, f32[16,64,128]{2,1,0:T(8,128)S(1)}, u32[]{:S(2)}, u32[]{:S(2)}) collective-permute-start(f32[16,64,128]{2,1,0:T(8,128)S(1)} %multiply_add_fusion.2), channel_id=1, source_target_pairs={{0,16},{16,32},{32,48},{48,64},{64,80},{80,96},{96,112},{112,128},... | collective-permute-start | bytes 1572872 | tf_op jit(solution)/shard_map/while/body/eval_jaxpr/ppermute | solution.py:16
  297.3 17.2 %collective-permute-start = (f32[16,64,128]{2,1,0:T(8,128)S(1)}, f32[16,64,128]{2,1,0:T(8,128)S(1)}, u32[]{:S(2)}, u32[]{:S(2)}) collective-permute-start(f32[16,64,128]{2,1,0:T(8,128)S(1)} %multiply_add_fusion.2), channel_id=1, source_target_pairs={{0,16},{16,32},{32,48},{48,64},{64,80},{80,96},{96,112},{112,128},... | collective-permute-start | bytes 1572872 | tf_op jit(solution)/shard_map/while/body/eval_jaxpr/ppermute | solution.py:16
  314.6 17.2 %collective-permute-start = (f32[16,64,128]{2,1,0:T(8,128)S(1)}, f32[16,64,128]{2,1,0:T(8,128)S(1)}, u32[]{:S(2)}, u32[]{:S(2)}) collective-permute-start(f32[16,64,128]{2,1,0:T(8,128)S(1)} %multiply_add_fusion.2), channel_id=1, source_target_pairs={{0,16},{16,32},{32,48},{48,64},{64,80},{80,96},{96,112},{112,128},... | collective-permute-start | bytes 1572872 | tf_op jit(solution)/shard_map/while/body/eval_jaxpr/ppermute | solution.py:16
  332.0 16.4 %collective-permute-start = (f32[16,64,128]{2,1,0:T(8,128)S(1)}, f32[16,64,128]{2,1,0:T(8,128)S(1)}, u32[]{:S(2)}, u32[]{:S(2)}) collective-permute-start(f32[16,64,128]{2,1,0:T(8,128)S(1)} %multiply_add_fusion.2), channel_id=1, source_target_pairs={{0,16},{16,32},{32,48},{48,64},{64,80},{80,96},{96,112},{112,128},... | collective-permute-start | bytes 1572872 | tf_op jit(solution)/shard_map/while/body/eval_jaxpr/ppermute | solution.py:16
  348.5 15.5 %collective-permute-start = (f32[16,64,128]{2,1,0:T(8,128)S(1)}, f32[16,64,128]{2,1,0:T(8,128)S(1)}, u32[]{:S(2)}, u32[]{:S(2)}) collective-permute-start(f32[16,64,128]{2,1,0:T(8,128)S(1)} %multiply_add_fusion.2), channel_id=1, source_target_pairs={{0,16},{16,32},{32,48},{48,64},{64,80},{80,96},{96,112},{112,128},... | collective-permute-start | bytes 1572872 | tf_op jit(solution)/shard_map/while/body/eval_jaxpr/ppermute | solution.py:16
  378.8 54.5 %copy-start.4 = (f32[1024]{0:T(1024)S(1)}, f32[1024]{0:T(1024)}, u32[]{:S(2)}) copy-start(f32[1024]{0:T(1024)} %param.23) | copy-start | bytes 12292
where the time goes:
time: 440 us; the launch traced here: 438 us
  waiting for transfers between devices  191 us (43%)
  matrix products  75.2 us (17%)
  other arithmetic  51.5 us (12%)
  blocking collectives  42.5 us (10%)
  local copies, waits for them, and re-layouts  41.4 us (9%)
  starting transfers between devices  36.3 us (8%)
    ppermute x17, waiting for transfers between devices, passed_along(): return lax.ppermute(block, axis, route)  191 us
    psum x1, blocking collectives, on_device(): squares = lax.psum(jnp.sum(gated_values * gated_values, axis=1), 'mp')  42.5 us
    ppermute x17, starting transfers between devices, passed_along(): return lax.ppermute(block, axis, route)  36.3 us
    dot_general x8, matrix products, block_pass(): jnp.einsum('hts,shp->thp', weights, per_head, precision=FULL_PRECISION)  26.8 us
    dot_general x8, matrix products, block_pass(): jnp.einsum('shp,sn->hpn', weighted, input_map, precision=FULL_PRECISION)  16.8 us
    dot_general x8, matrix products, block_pass(): jnp.einsum('tn,hpn->thp', output_map, state_now, precision=FULL_PRECISION)  15.2 us
    another operation x4, other arithmetic  13.8 us
    reduce_sum x1, other arithmetic, on_device(): squares = lax.psum(jnp.sum(gated_values * gated_values, axis=1), 'mp')  11.9 us
  transfers between devices with their start and end apart: 17, of which 15 were waited for; matrix products, arithmetic and copies ran while one was open for 5% of the time, Pallas kernels for 0%

commit v1 on v0

v1 whole, which is shorter than its diff:
```python
import functools
import math

import jax
import jax.numpy as jnp
import numpy as np
from jax import lax
from jax.experimental import pallas as pl
from jax.experimental.pallas import tpu as pltpu
from jax.sharding import PartitionSpec as P

CHUNK = 128
LANES = 128
HALO = 8
HEAD_DIM = 64
LOG2E = math.log2(math.e)
BF16 = jnp.bfloat16
F32 = jnp.float32


def params(mib):
    return pltpu.CompilerParams(vmem_limit_bytes=mib << 20)


def cost(flops, nbytes, trans=0):
    return pl.CostEstimate(flops=flops, bytes_accessed=nbytes, transcendentals=trans)


def silu(v):
    half = 0.5 * v
    return half + half * jnp.tanh(half)


def split(v):
    high = v.astype(BF16)
    return high, (v - high.astype(F32)).astype(BF16)


def contract_rows(a, b):
    return lax.dot_general(a, b, (((0,), (0,)), ((), ())), preferred_element_type=F32)


def contract_lanes(a, b):
    return lax.dot_general(a, b, (((1,), (1,)), ((), ())), preferred_element_type=F32)


def decay_kernel(raw_ref, mag_ref, tri_ref, row_ref, wtot_ref, ex_ref, dsec_ref):
    heads, tokens = raw_ref.shape
    chunks = tokens // CHUNK
    raw = raw_ref[...]
    small = jnp.exp(-jnp.abs(raw))
    grown = 1.0 + small
    rest = grown - 1.0
    safe = jnp.where(rest == 0.0, 1.0, rest)
    log1p = jnp.where(rest == 0.0, small, jnp.log(grown) * (small / safe))
    step = jnp.maximum(raw, 0.0) + log1p
    slope = -jnp.exp(mag_ref[...]) * LOG2E
    stacked = jnp.concatenate(
        [step[:, c * CHUNK : (c + 1) * CHUNK] for c in range(chunks)], axis=0
    )
    slopes = jnp.concatenate([slope] * chunks, axis=0)
    sums = jnp.dot(
        stacked * slopes, tri_ref[...], precision=lax.Precision.HIGHEST, preferred_element_type=F32
    )
    before = jnp.zeros((heads, 1), F32)
    befores, totals = [], []
    for c in range(chunks):
        befores.append(before)
        total = sums[c * heads : (c + 1) * heads, CHUNK - 1 : CHUNK]
        totals.append(total)
        before = before + total
    afters = [None] * chunks
    after = jnp.zeros((heads, 1), F32)
    for c in reversed(range(chunks)):
        afters[c] = after
        after = after + totals[c]
    for c in range(chunks):
        rows = slice(c * heads, (c + 1) * heads)
        upto = sums[rows, :CHUNK]
        beyond = sums[rows, CHUNK:]
        amount = stacked[rows]
        row_ref[c, 0:heads] = upto
        row_ref[c, heads : 2 * heads] = amount
        high, low = split(amount * jnp.exp2(beyond + afters[c]))
        wtot_ref[c, 0:heads] = high
        wtot_ref[c, heads : 2 * heads] = low
        for k, v in enumerate(
            (amount * jnp.exp2(beyond), jnp.exp2(upto), jnp.exp2(upto + befores[c]))
        ):
            high, low = split(v)
            ex_ref[c, (2 * k) * heads : (2 * k + 1) * heads] = high
            ex_ref[c, (2 * k + 1) * heads : (2 * k + 2) * heads] = low
    whole = jnp.broadcast_to(jnp.exp2(before), (heads, LANES))
    high, low = split(whole)
    lane = lax.broadcasted_iota(jnp.int32, (heads, LANES), 1)
    dsec_ref[0:heads] = jnp.where(lane == 0, high.astype(F32), 0.0).astype(BF16)
    dsec_ref[heads : 2 * heads] = jnp.where(lane == 1, low.astype(F32), 0.0).astype(BF16)


def mixed(ext_ref, tile, length, taps, bias):
    start = HALO - 3
    running = jnp.broadcast_to(bias, (length, LANES))
    for k in range(4):
        running = running + taps[k : k + 1] * ext_ref[tile, start + k : start + k + length, :]
    return silu(running)


def ends_kernel(
    feat_ref, coup_ref, halo_ref, taps_ref, bias_ref, ctaps_ref, cbias_ref, wtot_ref, dsec_ref, spread_ref,
    filt_ref, coupled_ref, pay_ref, ext_ref, weighted_ref, acc_ref,
):
    i = pl.program_id(0)
    length, channels = feat_ref.shape
    tiles = channels // LANES
    ctiles = coup_ref.shape[1] // LANES

    @pl.when(i == 0)
    def _():
        for j in range(tiles + ctiles):
            ext_ref[j, 0:HALO, :] = halo_ref[:, j * LANES : (j + 1) * LANES].astype(F32)
        acc_ref[...] = jnp.zeros_like(acc_ref)

    @pl.when(i > 0)
    def _():
        for j in range(tiles + ctiles):
            ext_ref[j, 0:HALO, :] = ext_ref[j, length : length + HALO, :]

    for j in range(ctiles):
        lanes = slice(j * LANES, (j + 1) * LANES)
        ext_ref[tiles + j, HALO : HALO + length, :] = coup_ref[:, lanes].astype(F32)
        coupled_ref[:, lanes] = mixed(
            ext_ref, tiles + j, length, ctaps_ref[:, lanes], cbias_ref[:, lanes]
        ).astype(BF16)
    for j in range(tiles):
        lanes = slice(j * LANES, (j + 1) * LANES)
        ext_ref[j, HALO : HALO + length, :] = feat_ref[:, lanes].astype(F32)
        value = mixed(ext_ref, j, length, taps_ref[:, lanes], bias_ref[:, lanes]).astype(BF16)
        filt_ref[:, lanes] = value
    for c in range(length // CHUNK):
        rows = slice(c * CHUNK, (c + 1) * CHUNK)
        scale = contract_rows(wtot_ref[c], spread_ref[...])
        weighted_ref[rows] = (filt_ref[rows].astype(F32) * scale).astype(BF16)
    acc_ref[...] += contract_rows(coupled_ref[:, :LANES], weighted_ref[...])

    @pl.when(i == pl.num_programs(0) - 1)
    def _():
        decays = contract_rows(dsec_ref[...], spread_ref[...])[0:8].astype(BF16)
        parts = pay_ref.shape[0]
        share = LANES // parts
        for j in range(parts):
            pay_ref[j, 0:share] = acc_ref[j * share : (j + 1) * share].astype(BF16)
            pay_ref[j, share : share + 8] = decays


def relay_kernel(pay_ref, order_ref, out_ref):
    parts, rows, _ = pay_ref.shape
    share = rows - 8
    entering = jnp.zeros(out_ref.shape[1:], F32)
    for j in range(parts):
        out_ref[j] = entering.astype(BF16)
        tail = pay_ref[j, share : share + 8].astype(F32)
        decay = tail[0:1] + tail[1:2]
        entering = decay * entering + pay_ref[j, 0:share].astype(F32)


def inside_kernel(
    filt_ref, coupled_ref, gate_ref, row_ref, ex_ref, spread_ref, state_ref, order_ref, *rest
):
    yg_ref, gp_ref, end_ref, narrow_ref = rest[-4:]
    i = pl.program_id(0)
    heads = row_ref.shape[1] // 2
    channels = filt_ref.shape[1]

    @pl.when(i == 0)
    def _():
        end_ref[...] = state_ref[...]

    inputs = coupled_ref[:, :LANES]
    reads = coupled_ref[:, LANES:]
    above = lax.broadcasted_iota(jnp.int32, (CHUNK, CHUNK), 0)
    below = lax.broadcasted_iota(jnp.int32, (CHUNK, CHUNK), 1)
    scores = jnp.where(above >= below, contract_lanes(reads, inputs), 0.0)
    rows = row_ref[0, 0:heads]
    amounts = row_ref[0, heads : 2 * heads]
    columns = rows.T
    lane = lax.broadcasted_iota(jnp.int32, (1, LANES), 1)
    left = jnp.where(lane < HEAD_DIM, 1.0, 0.0)
    right = 1.0 - left
    narrow_ref[...] = end_ref[...].astype(BF16)
    width = 2 * LANES
    for q in range(channels // width):
        lanes = slice(q * width, (q + 1) * width)
        spread = spread_ref[:, lanes]
        x = filt_ref[:, lanes].astype(F32)
        decayed = contract_rows(ex_ref[0, 2 * heads : 4 * heads], spread)
        carried = jnp.dot(reads, narrow_ref[:, lanes], preferred_element_type=F32) * decayed
        last = decayed[CHUNK - 1 : CHUNK]
        weighted = (x * contract_rows(ex_ref[0, 0 : 2 * heads], spread)).astype(BF16)
        end_ref[:, lanes] = end_ref[:, lanes] * last + contract_rows(inputs, weighted)
        parts = []
        for p in range(2):
            weights = []
            for h in (4 * q + 2 * p, 4 * q + 2 * p + 1):
                gap = jnp.minimum(columns[:, h : h + 1] - rows[h : h + 1], 0.0)
                weights.append((jnp.exp2(gap) * scores * amounts[h : h + 1]).astype(BF16))
            pair = x[:, p * LANES : (p + 1) * LANES]
            block = jnp.concatenate([(pair * left).astype(BF16), (pair * right).astype(BF16)], axis=0)
            parts.append(
                jnp.dot(jnp.concatenate(weights, axis=1), block, preferred_element_type=F32)
            )
        total = carried + jnp.concatenate(parts, axis=1)
        opened = silu(gate_ref[:, lanes].astype(F32))
        yg_ref[:, lanes] = (total * opened).astype(BF16)
        running = contract_rows(ex_ref[0, 4 * heads : 6 * heads], spread)
        gp_ref[:, lanes] = (opened * running).astype(BF16)


def gated_kernel(read_ref, enter_ref, yg_ref, gp_ref, gated_ref, out_ref, sums_ref):
    i = pl.program_id(0)
    length, channels = yg_ref.shape
    before = jnp.dot(read_ref[...], enter_ref[...], preferred_element_type=F32)
    gated = yg_ref[...].astype(F32) + gp_ref[...].astype(F32) * before
    gated_ref[...] = gated.astype(BF16)
    ones = jnp.ones((8, channels), BF16)
    squares = contract_lanes(ones, (gated * gated).astype(BF16))
    for c in range(length // CHUNK):
        sums_ref[pl.ds(i * (length // CHUNK) + c, 1), :] = squares[0:1, c * CHUNK : (c + 1) * CHUNK]

    @pl.when(i == pl.num_programs(0) - 1)
    def _():
        mine = sums_ref[...].astype(out_ref.dtype)
        for j in range(out_ref.shape[0]):
            out_ref[j] = mine


def normal_kernel(inner, gated_ref, sums_ref, gain_ref, out_ref, scale_ref):
    i = pl.program_id(0)
    length, channels = gated_ref.shape
    chunks = sums_ref.shape[1]

    @pl.when(i == 0)
    def _():
        total = sums_ref[0].astype(F32)
        for j in range(1, sums_ref.shape[0]):
            total = total + sums_ref[j].astype(F32)
        columns = lax.rsqrt(total / inner + 1e-05).T
        for c in range(chunks):
            scale_ref[c] = jnp.broadcast_to(columns[:, c : c + 1], (CHUNK, LANES))

    per = length // CHUNK
    for c in range(per):
        rows = slice(c * CHUNK, (c + 1) * CHUNK)
        scale = scale_ref[i * per + c]
        for j in range(channels // LANES):
            lanes = slice(j * LANES, (j + 1) * LANES)
            out_ref[rows, lanes] = (
                gated_ref[rows, lanes].astype(F32) * gain_ref[:, lanes] * scale
            ).astype(BF16)


def whole(shape):
    return pl.BlockSpec(shape, lambda i: (0,) * len(shape))


def on_device(
    features,
    coupling,
    gate_values,
    step_raw,
    decay_log,
    feature_taps,
    feature_offset,
    coupling_taps,
    coupling_offset,
    norm_gain,
):
    tokens, channels = features.shape
    heads = decay_log.shape[0]
    sections = lax.axis_size("seq")
    groups = lax.axis_size("mp")
    chunks = tokens // CHUNK
    share = LANES // sections
    any_spec = pl.BlockSpec(memory_space=pl.ANY)

    tail = jnp.concatenate([features[tokens - HALO :], coupling[tokens - HALO :]], axis=1)
    halo = lax.ppermute(tail, "seq", [(i, i + 1) for i in range(sections - 1)])

    order = np.arange(CHUNK)
    tri = np.concatenate(
        [order[:, None] <= order[None, :], order[:, None] > order[None, :]], axis=1
    ).astype(np.float32)
    one = np.arange(channels)[None, :] // HEAD_DIM == np.arange(heads)[:, None]
    spread = jnp.asarray(np.concatenate([one, one], axis=0), BF16)

    rows, wtot, ex, dsec = pl.pallas_call(
        decay_kernel,
        out_shape=(
            jax.ShapeDtypeStruct((chunks, 2 * heads, CHUNK), F32),
            jax.ShapeDtypeStruct((chunks, 2 * heads, CHUNK), BF16),
            jax.ShapeDtypeStruct((chunks, 6 * heads, CHUNK), BF16),
            jax.ShapeDtypeStruct((2 * heads, LANES), BF16),
        ),
        compiler_params=params(8),
        cost_estimate=cost(10**7, 10**6, 10**5),
    )(step_raw, decay_log[:, None], jnp.asarray(tri))

    block = 2 * CHUNK
    filtered, coupled, ends = pl.pallas_call(
        ends_kernel,
        grid=(tokens // block,),
        in_specs=[
            pl.BlockSpec((block, channels), lambda i: (i, 0)),
            pl.BlockSpec((block, 2 * LANES), lambda i: (i, 0)),
            whole((HALO, channels + 2 * LANES)),
            whole((4, channels)),
            whole((1, channels)),
            whole((4, 2 * LANES)),
            whole((1, 2 * LANES)),
            pl.BlockSpec((2, 2 * heads, CHUNK), lambda i: (i, 0, 0)),
            whole((2 * heads, LANES)),
            whole((2 * heads, channels)),
        ],
        out_specs=(
            pl.BlockSpec((block, channels), lambda i: (i, 0)),
            pl.BlockSpec((block, 2 * LANES), lambda i: (i, 0)),
            whole((sections, share + 8, channels)),
        ),
        out_shape=(
            jax.ShapeDtypeStruct((tokens, channels), BF16),
            jax.ShapeDtypeStruct((tokens, 2 * LANES), BF16),
            jax.ShapeDtypeStruct((sections, share + 8, channels), BF16),
        ),
        scratch_shapes=[
            pltpu.VMEM((channels // LANES + 2, HALO + block, LANES), F32),
            pltpu.VMEM((block, channels), BF16),
            pltpu.VMEM((LANES, channels), F32),
        ],
        compiler_params=params(24),
        cost_estimate=cost(10**9, 10**7, 2 * 10**6),
    )(
        features,
        coupling,
        halo,
        feature_taps,
        feature_offset[None, :],
        coupling_taps,
        coupling_offset[None, :],
        wtot,
        dsec,
        spread,
    )

    def inside(first, count, state, order, *held):
        return pl.pallas_call(
            inside_kernel,
            grid=(count,),
            in_specs=[
                pl.BlockSpec((CHUNK, channels), lambda i: (first + i, 0)),
                pl.BlockSpec((CHUNK, 2 * LANES), lambda i: (first + i, 0)),
                pl.BlockSpec((CHUNK, channels), lambda i: (first + i, 0)),
                pl.BlockSpec((1, 2 * heads, CHUNK), lambda i: (first + i, 0, 0)),
                pl.BlockSpec((1, 6 * heads, CHUNK), lambda i: (first + i, 0, 0)),
                whole((2 * heads, channels)),
                whole((LANES, channels)),
                any_spec,
            ]
            + [any_spec] * len(held),
            out_specs=(
                pl.BlockSpec((CHUNK, channels), lambda i: (first + i, 0)),
                pl.BlockSpec((CHUNK, channels), lambda i: (first + i, 0)),
                whole((LANES, channels)),
            ),
            out_shape=(
                jax.ShapeDtypeStruct((tokens, channels), BF16),
                jax.ShapeDtypeStruct((tokens, channels), BF16),
                jax.ShapeDtypeStruct((LANES, channels), F32),
            ),
            input_output_aliases={8 + k: k for k in range(len(held))},
            scratch_shapes=[pltpu.VMEM((LANES, channels), BF16)],
            compiler_params=params(24),
            cost_estimate=cost(count * 3 * 10**8, count * 10**6, count * 4 * 10**5),
        )(filtered, coupled, gate_values, rows, ex, spread, state, order, *held)

    half = chunks // 2
    gathered = lax.all_to_all(ends, "seq", 0, 0, tiled=True)
    yg, gp, state = inside(0, half, jnp.zeros((LANES, channels), F32), dsec)
    starts = pl.pallas_call(
        relay_kernel,
        grid=(1,),
        in_specs=[whole((sections, share + 8, channels)), any_spec],
        out_specs=whole((sections, share, channels)),
        out_shape=jax.ShapeDtypeStruct((sections, share, channels), BF16),
        compiler_params=params(8),
        cost_estimate=cost(10**6, 10**6),
    )(gathered, state)
    entering = lax.all_to_all(starts, "seq", 0, 0, tiled=True).reshape(LANES, channels)
    yg, gp, _ = inside(half, chunks - half, state, starts, yg, gp)

    gated, squares = pl.pallas_call(
        gated_kernel,
        grid=(tokens // block,),
        in_specs=[
            pl.BlockSpec((block, LANES), lambda i: (i, 1)),
            whole((LANES, channels)),
            pl.BlockSpec((block, channels), lambda i: (i, 0)),
            pl.BlockSpec((block, channels), lambda i: (i, 0)),
        ],
        out_specs=(
            pl.BlockSpec((block, channels), lambda i: (i, 0)),
            whole((groups, chunks, CHUNK)),
        ),
        out_shape=(
            jax.ShapeDtypeStruct((tokens, channels), BF16),
            jax.ShapeDtypeStruct((groups, chunks, CHUNK), F32),
        ),
        scratch_shapes=[pltpu.VMEM((chunks, CHUNK), F32)],
        compiler_params=params(16),
        cost_estimate=cost(6 * 10**8, 12 * 10**6),
    )(coupled, entering, yg, gp)
    squares = lax.all_to_all(squares, "mp", 0, 0, tiled=True)

    return pl.pallas_call(
        functools.partial(normal_kernel, float(channels * groups)),
        grid=(tokens // block,),
        in_specs=[
            pl.BlockSpec((block, channels), lambda i: (i, 0)),
            whole((groups, chunks, CHUNK)),
            whole((1, channels)),
        ],
        out_specs=pl.BlockSpec((block, channels), lambda i: (i, 0)),
        out_shape=jax.ShapeDtypeStruct((tokens, channels), BF16),
        scratch_shapes=[pltpu.VMEM((chunks, CHUNK, LANES), F32)],
        compiler_params=params(16),
        cost_estimate=cost(10**7, 8 * 10**6),
    )(gated, squares, norm_gain[None, :])


def solution(mesh):
    in_specs = (
        P("seq", "mp"),
        P("seq", None),
        P("seq", "mp"),
        P("mp", "seq"),
        P("mp"),
        P(None, "mp"),
        P("mp"),
        P(),
        P(),
        P("mp"),
    )
    out_specs = P("seq", "mp")
    return jax.shard_map(
        on_device, mesh=mesh, in_specs=in_specs, out_specs=out_specs, check_vma=False
    )
```

time: 440 us -> 120 us (0.27)
  the two profiles are of different devices: /device:TPU:7 before, /device:TPU:1 now
where the time goes in v1:
time: 120 us; the launch traced here: 119 us
  Pallas kernels  44 us (37%)
  local copies, waits for them, and re-layouts  38.5 us (32%)
  blocking collectives  19 us (16%)
  starting transfers between devices  17.1 us (14%)
    unnamed x48, local copies, waits for them, and re-layouts  36.3 us
    pallas_call x2, Pallas kernels, inside(): pl.pallas_call(inside_kernel, grid=(count,), in_specs=[pl.BlockSpec((CHUN...  22.8 us
    all_to_all x1, blocking collectives, on_device(): squares = lax.all_to_all(squares, 'mp', 0, 0, tiled=True)  19 us
    pallas_call x1, Pallas kernels, on_device(): pl.pallas_call(ends_kernel, grid=(tokens // block,), in_specs=[pl.BlockSp...  10.9 us
    all_to_all x1, starting transfers between devices, on_device(): lax.all_to_all(starts, 'seq', 0, 0, tiled=True).reshape(LANES, channels)  6.65 us
    all_to_all x1, starting transfers between devices, on_device(): gathered = lax.all_to_all(ends, 'seq', 0, 0, tiled=True)  6.46 us
    pallas_call x1, Pallas kernels, on_device(): pl.pallas_call(gated_kernel, grid=(tokens // block,), in_specs=[pl.BlockS...  4.52 us
    pallas_call x1, Pallas kernels, on_device(): pl.pallas_call(functools.partial(normal_kernel, float(channels * groups))...  4.47 us
  transfers between devices with their start and end apart: 3, of which 0 were waited for; matrix products, arithmetic and copies ran while one was open for 1% of the time, Pallas kernels for 20%

profile of v1, /device:TPU:1, one launch (start us, length us, event | category | flops | bytes accessed | tf_op | source)
XLA Modules:
  0.0 118.7 jit_solution(10763936981541533303)
XLA Ops:
  1.4 4.0 %collective-permute-start = (bf16[8,1280]{1,0:T(8,128)(2,1)S(1)}, bf16[8,1280]{1,0:T(8,128)(2,1)S(1)}, u32[]{:S(2)}, u32[]{:S(2)}) collective-permute-start(bf16[8,1280]{1,0:T(8,128)(2,1)S(1)} %pad_maximum_fusion), channel_id=1, source_target_pairs={{0,16},{16,32},{32,48},{48,64},{64,80},{80,96},{96,112},{112,128},... | collective-permute-start | bytes 61448 | tf_op jit(solution)/shard_map/ppermute | solution.py:286
  8.6 2.2 %copy-done.13 = bf16[2048,1024]{1,0:T(8,128)(2,1)S(1)} copy-done((bf16[2048,1024]{1,0:T(8,128)(2,1)S(1)}, bf16[2048,1024]{1,0:T(8,128)(2,1)}, u32[]{:S(2)}) %copy-start.13) | copy-done | bytes 4194328
  10.7 1.2 %copy-done.14 = bf16[2048,256]{1,0:T(8,128)(2,1)S(1)} copy-done((bf16[2048,256]{1,0:T(8,128)(2,1)S(1)}, bf16[2048,256]{1,0:T(8,128)(2,1)}, u32[]{:S(2)}) %copy-start.14) | copy-done | bytes 1048600
  15.6 10.9 %shard_map.119 = (bf16[2048,1024]{1,0:T(8,128)(2,1)S(1)}, bf16[2048,256]{1,0:T(8,128)(2,1)S(1)}, bf16[16,16,1024]{2,1,0:T(8,128)(2,1)}) custom-call(bf16[2048,1024]{1,0:T(8,128)(2,1)S(1)} %copy-done.13, bf16[2048,256]{1,0:T(8,128)(2,1)S(1)} %copy-done.14, bf16[8,1280]{1,0:T(8,128)(2,1)S(1)} %collective-permute-done.halo_ref, f32[4,1024]{1,0:T(4,128)S(1)} %copy-done.19, ...), custom_call_target="tpu_custom_call" | custom-call | flops 1000000000 | bytes 10000000 | tf_op jit(solution)/shard_map/pallas_call | solution.py:308
  26.4 2.0 %copy-done.10 = bf16[2048,1024]{1,0:T(8,128)(2,1)} copy-done((bf16[2048,1024]{1,0:T(8,128)(2,1)}, bf16[2048,1024]{1,0:T(8,128)(2,1)S(1)}, u32[]{:S(2)}) %copy-start.10) | copy-done | bytes 4194328
  28.5 6.5 %all-to-all-start = ((bf16[16,16,1024]{2,1,0:T(8,128)(2,1)}), bf16[16,16,1024]{2,1,0:T(8,128)(2,1)S(1)}, u32[]{:S(2)}, u32[]{:S(2)}) async-start(bf16[16,16,1024]{2,1,0:T(8,128)(2,1)} %get-tuple-element.22), calls=%async_computation | async-start | bytes 1048576 | tf_op jit(solution)/shard_map/all_to_all | solution.py:385
  35.0 2.2 %copy-done.8 = bf16[2048,1024]{1,0:T(8,128)(2,1)S(1)} copy-done((bf16[2048,1024]{1,0:T(8,128)(2,1)S(1)}, bf16[2048,1024]{1,0:T(8,128)(2,1)}, u32[]{:S(2)}) %copy-start.8) | copy-done | bytes 4194328
  37.2 2.2 %copy-done.11 = bf16[2048,1024]{1,0:T(8,128)(2,1)S(1)} copy-done((bf16[2048,1024]{1,0:T(8,128)(2,1)S(1)}, bf16[2048,1024]{1,0:T(8,128)(2,1)}, u32[]{:S(2)}) %copy-start.11) | copy-done | bytes 4194328
  39.4 11.0 %shard_map.120 = (bf16[2048,1024]{1,0:T(8,128)(2,1)S(1)}, bf16[2048,1024]{1,0:T(8,128)(2,1)S(1)}, f32[128,1024]{1,0:T(8,128)S(1)}) custom-call(bf16[2048,1024]{1,0:T(8,128)(2,1)S(1)} %copy-done.11, bf16[2048,256]{1,0:T(8,128)(2,1)S(1)} %get-tuple-element.21.coupled_ref.read_ref, bf16[2048,1024]{1,0:T(8,128)(2,1)S(1)} %copy-done.8, ...), custom_call_target="tpu_custom_call" | custom-call | flops 2400000000 | bytes 8000000 | tf_op jit(solution)/shard_map/pallas_call | solution.py:354
  50.4 1.9 %copy-done = bf16[2048,1024]{1,0:T(8,128)(2,1)} copy-done((bf16[2048,1024]{1,0:T(8,128)(2,1)}, bf16[2048,1024]{1,0:T(8,128)(2,1)S(1)}, u32[]{:S(2)}) %copy-start) | copy-done | bytes 4194328
  52.4 2.0 %copy-done.4 = bf16[2048,1024]{1,0:T(8,128)(2,1)} copy-done((bf16[2048,1024]{1,0:T(8,128)(2,1)}, bf16[2048,1024]{1,0:T(8,128)(2,1)S(1)}, u32[]{:S(2)}) %copy-start.4) | copy-done | bytes 4194328
  55.2 6.7 %all-to-all-start.1 = ((bf16[16,8,1024]{2,1,0:T(8,128)(2,1)}), bf16[16,8,1024]{2,1,0:T(8,128)(2,1)S(1)}, u32[]{:S(2)}, u32[]{:S(2)}) async-start(bf16[16,8,1024]{2,1,0:T(8,128)(2,1)} %shard_map.121.order_ref), calls=%async_computation.1 | async-start | bytes 524288 | tf_op jit(solution)/shard_map/all_to_all | solution.py:396
  61.9 2.2 %copy-done.1 = bf16[2048,1024]{1,0:T(8,128)(2,1)S(1)} copy-done((bf16[2048,1024]{1,0:T(8,128)(2,1)S(1)}, bf16[2048,1024]{1,0:T(8,128)(2,1)}, u32[]{:S(2)}) %copy-start.1) | copy-done | bytes 4194328
  64.1 2.2 %copy-done.5 = bf16[2048,1024]{1,0:T(8,128)(2,1)S(1)} copy-done((bf16[2048,1024]{1,0:T(8,128)(2,1)S(1)}, bf16[2048,1024]{1,0:T(8,128)(2,1)}, u32[]{:S(2)}) %copy-start.5) | copy-done | bytes 4194328
  66.3 2.2 %copy-done.9 = bf16[2048,1024]{1,0:T(8,128)(2,1)S(1)} copy-done((bf16[2048,1024]{1,0:T(8,128)(2,1)S(1)}, bf16[2048,1024]{1,0:T(8,128)(2,1)}, u32[]{:S(2)}) %copy-start.9) | copy-done | bytes 4194328
  68.5 2.2 %copy-done.12 = bf16[2048,1024]{1,0:T(8,128)(2,1)S(1)} copy-done((bf16[2048,1024]{1,0:T(8,128)(2,1)S(1)}, bf16[2048,1024]{1,0:T(8,128)(2,1)}, u32[]{:S(2)}) %copy-start.12) | copy-done | bytes 4194328
  70.6 11.7 %shard_map.122 = (bf16[2048,1024]{1,0:T(8,128)(2,1)S(1)}, bf16[2048,1024]{1,0:T(8,128)(2,1)S(1)}, f32[128,1024]{1,0:T(8,128)}) custom-call(bf16[2048,1024]{1,0:T(8,128)(2,1)S(1)} %copy-done.12, bf16[2048,256]{1,0:T(8,128)(2,1)S(1)} %get-tuple-element.21.coupled_ref.read_ref, ...), custom_call_target="tpu_custom_call", output_to_operand_aliasing={{0}: (8, {}), {1}: (9, {})} | custom-call | flops 2400000000 | bytes 8000000 | tf_op jit(solution)/shard_map/pallas_call | solution.py:354
  82.4 2.0 %copy-done.2 = bf16[2048,1024]{1,0:T(8,128)(2,1)} copy-done((bf16[2048,1024]{1,0:T(8,128)(2,1)}, bf16[2048,1024]{1,0:T(8,128)(2,1)S(1)}, u32[]{:S(2)}) %copy-start.2) | copy-done | bytes 4194328
  84.4 2.0 %copy-done.6 = bf16[2048,1024]{1,0:T(8,128)(2,1)} copy-done((bf16[2048,1024]{1,0:T(8,128)(2,1)}, bf16[2048,1024]{1,0:T(8,128)(2,1)S(1)}, u32[]{:S(2)}) %copy-start.6) | copy-done | bytes 4194328
  86.4 2.2 %copy-done.3 = bf16[2048,1024]{1,0:T(8,128)(2,1)S(1)} copy-done((bf16[2048,1024]{1,0:T(8,128)(2,1)S(1)}, bf16[2048,1024]{1,0:T(8,128)(2,1)}, u32[]{:S(2)}) %copy-start.3) | copy-done | bytes 4194328
  88.5 2.2 %copy-done.7 = bf16[2048,1024]{1,0:T(8,128)(2,1)S(1)} copy-done((bf16[2048,1024]{1,0:T(8,128)(2,1)S(1)}, bf16[2048,1024]{1,0:T(8,128)(2,1)}, u32[]{:S(2)}) %copy-start.7) | copy-done | bytes 4194328
  90.7 4.5 %shard_map.123 = (bf16[2048,1024]{1,0:T(8,128)(2,1)S(1)}, f32[16,16,128]{2,1,0:T(8,128)S(1)}) custom-call(bf16[2048,256]{1,0:T(8,128)(2,1)S(1)} %get-tuple-element.21.coupled_ref.read_ref, bf16[128,1024]{1,0:T(8,128)(2,1)S(1)} %bitcast.5, bf16[2048,1024]{1,0:T(8,128)(2,1)S(1)} %copy-done.3, bf16[2048,1024]{1,0:T(8,128)(2,1)S(1)} %copy-done.7), custom_call_target="tpu_custom_call" | custom-call | flops 600000000 | bytes 12000000 | tf_op jit(solution)/shard_map/pallas_call | solution.py:399
  95.3 19.0 %all_to_all.15.sums_ref = f32[16,16,128]{2,1,0:T(8,128)S(1)} all-to-all(f32[16,16,128]{2,1,0:T(8,128)S(1)} %get-tuple-element.32), channel_id=1, replica_groups=mesh['seq'=16,'mp'=16] {'mp'}, dimensions={0} | all-to-all | bytes 262144 | tf_op jit(solution)/shard_map/all_to_all | solution.py:420
  114.2 4.5 %shard_map.124 = bf16[2048,1024]{1,0:T(8,128)(2,1)} custom-call(bf16[2048,1024]{1,0:T(8,128)(2,1)S(1)} %get-tuple-element.31.gated_ref, f32[16,16,128]{2,1,0:T(8,128)S(1)} %all_to_all.15.sums_ref, f32[1,1024]{1,0:T(1,128)S(1)} %bitcast.6), custom_call_target="tpu_custom_call" | custom-call | flops 10000000 | bytes 8000000 | tf_op jit(solution)/shard_map/pallas_call | solution.py:422
  (43 shorter events, 9.1 us)
Async XLA Ops:
  0.0 35.0 %copy-start.16 = (bf16[32,1024]{1,0:T(8,128)(2,1)S(1)}, bf16[32,1024]{1,0:T(8,128)(2,1)}, u32[]{:S(2)}) copy-start(bf16[32,1024]{1,0:T(8,128)(2,1)} %constant.6.clone.spread_ref) | copy-start | bytes 196612
  1.4 7.1 %collective-permute-start = (bf16[8,1280]{1,0:T(8,128)(2,1)S(1)}, bf16[8,1280]{1,0:T(8,128)(2,1)S(1)}, u32[]{:S(2)}, u32[]{:S(2)}) collective-permute-start(bf16[8,1280]{1,0:T(8,128)(2,1)S(1)} %pad_maximum_fusion), channel_id=1, source_target_pairs={{0,16},{16,32},{32,48},{48,64},{64,80},{80,96},{96,112},{112,128},... | collective-permute-start | bytes 61448 | tf_op jit(solution)/shard_map/ppermute | solution.py:286
  6.2 0.9 copy-start.17
  7.1 0.9 copy-start.18
  8.6 2.2 %copy-start.13 = (bf16[2048,1024]{1,0:T(8,128)(2,1)S(1)}, bf16[2048,1024]{1,0:T(8,128)(2,1)}, u32[]{:S(2)}) copy-start(bf16[2048,1024]{1,0:T(8,128)(2,1)} %feat_ref.1) | copy-start | bytes 12582916
  10.7 1.2 %copy-start.14 = (bf16[2048,256]{1,0:T(8,128)(2,1)S(1)}, bf16[2048,256]{1,0:T(8,128)(2,1)}, u32[]{:S(2)}) copy-start(bf16[2048,256]{1,0:T(8,128)(2,1)} %coup_ref.1) | copy-start | bytes 3145732
  12.0 0.8 copy-start.15
  12.8 0.7 copy-start.19
  26.4 2.0 %copy-start.10 = (bf16[2048,1024]{1,0:T(8,128)(2,1)}, bf16[2048,1024]{1,0:T(8,128)(2,1)S(1)}, u32[]{:S(2)}) copy-start(bf16[2048,1024]{1,0:T(8,128)(2,1)S(1)} %get-tuple-element.23.filt_ref) | copy-start | bytes 12582916
  28.5 25.9 %all-to-all-start = ((bf16[16,16,1024]{2,1,0:T(8,128)(2,1)}), bf16[16,16,1024]{2,1,0:T(8,128)(2,1)S(1)}, u32[]{:S(2)}, u32[]{:S(2)}) async-start(bf16[16,16,1024]{2,1,0:T(8,128)(2,1)} %get-tuple-element.22), calls=%async_computation | async-start | bytes 1048576 | tf_op jit(solution)/shard_map/all_to_all | solution.py:385
  35.0 2.2 %copy-start.8 = (bf16[2048,1024]{1,0:T(8,128)(2,1)S(1)}, bf16[2048,1024]{1,0:T(8,128)(2,1)}, u32[]{:S(2)}) copy-start(bf16[2048,1024]{1,0:T(8,128)(2,1)} %gate_ref.3) | copy-start | bytes 12582916
  37.2 2.2 %copy-start.11 = (bf16[2048,1024]{1,0:T(8,128)(2,1)S(1)}, bf16[2048,1024]{1,0:T(8,128)(2,1)}, u32[]{:S(2)}) copy-start(bf16[2048,1024]{1,0:T(8,128)(2,1)} %copy-done.10) | copy-start | bytes 12582916
  50.4 2.0 %copy-start = (bf16[2048,1024]{1,0:T(8,128)(2,1)}, bf16[2048,1024]{1,0:T(8,128)(2,1)S(1)}, u32[]{:S(2)}) copy-start(bf16[2048,1024]{1,0:T(8,128)(2,1)S(1)} %get-tuple-element.27.rest_0_) | copy-start | bytes 12582916
  52.4 2.0 %copy-start.4 = (bf16[2048,1024]{1,0:T(8,128)(2,1)}, bf16[2048,1024]{1,0:T(8,128)(2,1)S(1)}, u32[]{:S(2)}) copy-start(bf16[2048,1024]{1,0:T(8,128)(2,1)S(1)} %get-tuple-element.28.rest_1_) | copy-start | bytes 12582916
  55.2 31.1 %all-to-all-start.1 = ((bf16[16,8,1024]{2,1,0:T(8,128)(2,1)}), bf16[16,8,1024]{2,1,0:T(8,128)(2,1)S(1)}, u32[]{:S(2)}, u32[]{:S(2)}) async-start(bf16[16,8,1024]{2,1,0:T(8,128)(2,1)} %shard_map.121.order_ref), calls=%async_computation.1 | async-start | bytes 524288 | tf_op jit(solution)/shard_map/all_to_all | solution.py:396
  61.9 2.2 %copy-start.1 = (bf16[2048,1024]{1,0:T(8,128)(2,1)S(1)}, bf16[2048,1024]{1,0:T(8,128)(2,1)}, u32[]{:S(2)}) copy-start(bf16[2048,1024]{1,0:T(8,128)(2,1)} %copy-done) | copy-start | bytes 12582916
  64.1 2.2 %copy-start.5 = (bf16[2048,1024]{1,0:T(8,128)(2,1)S(1)}, bf16[2048,1024]{1,0:T(8,128)(2,1)}, u32[]{:S(2)}) copy-start(bf16[2048,1024]{1,0:T(8,128)(2,1)} %copy-done.4) | copy-start | bytes 12582916
  66.3 2.2 %copy-start.9 = (bf16[2048,1024]{1,0:T(8,128)(2,1)S(1)}, bf16[2048,1024]{1,0:T(8,128)(2,1)}, u32[]{:S(2)}) copy-start(bf16[2048,1024]{1,0:T(8,128)(2,1)} %gate_ref.3) | copy-start | bytes 12582916
  68.4 2.2 %copy-start.12 = (bf16[2048,1024]{1,0:T(8,128)(2,1)S(1)}, bf16[2048,1024]{1,0:T(8,128)(2,1)}, u32[]{:S(2)}) copy-start(bf16[2048,1024]{1,0:T(8,128)(2,1)} %copy-done.10) | copy-start | bytes 12582916
  82.4 2.0 %copy-start.2 = (bf16[2048,1024]{1,0:T(8,128)(2,1)}, bf16[2048,1024]{1,0:T(8,128)(2,1)S(1)}, u32[]{:S(2)}) copy-start(bf16[2048,1024]{1,0:T(8,128)(2,1)S(1)} %get-tuple-element.29.yg_ref) | copy-start | bytes 12582916
  84.4 2.0 %copy-start.6 = (bf16[2048,1024]{1,0:T(8,128)(2,1)}, bf16[2048,1024]{1,0:T(8,128)(2,1)S(1)}, u32[]{:S(2)}) copy-start(bf16[2048,1024]{1,0:T(8,128)(2,1)S(1)} %get-tuple-element.30.gp_ref) | copy-start | bytes 12582916
  86.3 2.2 %copy-start.3 = (bf16[2048,1024]{1,0:T(8,128)(2,1)S(1)}, bf16[2048,1024]{1,0:T(8,128)(2,1)}, u32[]{:S(2)}) copy-start(bf16[2048,1024]{1,0:T(8,128)(2,1)} %copy-done.2) | copy-start | bytes 12582916
  88.5 2.2 %copy-start.7 = (bf16[2048,1024]{1,0:T(8,128)(2,1)S(1)}, bf16[2048,1024]{1,0:T(8,128)(2,1)}, u32[]{:S(2)}) copy-start(bf16[2048,1024]{1,0:T(8,128)(2,1)} %copy-done.6) | copy-start | bytes 12582916
  90.7 23.5 %copy-start.20 = (f32[1024]{0:T(1024)S(1)}, f32[1024]{0:T(1024)}, u32[]{:S(2)}) copy-start(f32[1024]{0:T(1024)} %param.21) | copy-start | bytes 12292
  (3 other events, 2.1 us)

commit v2 on v1

--- a/solution.py
+++ b/solution.py
@@ -19,7 +19,7 @@
 
 
 def params(mib):
-    return pltpu.CompilerParams(vmem_limit_bytes=mib << 20)
+    return pltpu.CompilerParams(vmem_limit_bytes=60 << 20)
 
 
 def cost(flops, nbytes, trans=0):

time: 120 us -> 104 us (0.87)
  local copies, waits for them, and re-layouts: 38.5 us -> 5.72 us
  Pallas kernels: 44 us -> 61 us
    unnamed x48 -> x6, local copies, waits for them, and re-layouts: 36.3 us -> 2.12 us
    pallas_call x1, Pallas kernels: 4.52 us -> 9.63 us  [on_device(): pl.pallas_call(gated_kernel, grid=(tokens // block,), in_specs=[pl.BlockS...]
    pallas_call x2, Pallas kernels: 22.8 us -> 27.2 us  [inside(): pl.pallas_call(inside_kernel, grid=(count,), in_specs=[pl.BlockSpec((CHUN...]
    pallas_call x1, Pallas kernels: 4.47 us -> 7.57 us  [on_device(): pl.pallas_call(functools.partial(normal_kernel, float(channels * groups))...]
    pallas_call x1, Pallas kernels: 0.53 us -> 2.29 us  [on_device(): pl.pallas_call(decay_kernel, out_shape=(jax.ShapeDtypeStruct((chunks, 2 *...]
    pallas_call x1, Pallas kernels: 10.9 us -> 12.5 us  [on_device(): pl.pallas_call(ends_kernel, grid=(tokens // block,), in_specs=[pl.BlockSp...]
  transfers between devices with their start and end apart: 3 -> 3, of which waited for: 0 -> 0; matrix products, arithmetic and copies ran while one was open for 1% -> 2% of each run, Pallas kernels for 20% -> 29%
where the time goes in v2:
time: 104 us; the launch traced here: 103 us
  Pallas kernels  61 us (59%)
  blocking collectives  19.3 us (19%)
  starting transfers between devices  17.1 us (16%)
  local copies, waits for them, and re-layouts  5.72 us (6%)
    pallas_call x2, Pallas kernels, inside(): pl.pallas_call(inside_kernel, grid=(count,), in_specs=[pl.BlockSpec((CHUN...  27.2 us
    all_to_all x1, blocking collectives, on_device(): squares = lax.all_to_all(squares, 'mp', 0, 0, tiled=True)  19.3 us
    pallas_call x1, Pallas kernels, on_device(): pl.pallas_call(ends_kernel, grid=(tokens // block,), in_specs=[pl.BlockSp...  12.5 us
    pallas_call x1, Pallas kernels, on_device(): pl.pallas_call(gated_kernel, grid=(tokens // block,), in_specs=[pl.BlockS...  9.63 us
    pallas_call x1, Pallas kernels, on_device(): pl.pallas_call(functools.partial(normal_kernel, float(channels * groups))...  7.57 us
    all_to_all x1, starting transfers between devices, on_device(): lax.all_to_all(starts, 'seq', 0, 0, tiled=True).reshape(LANES, channels)  6.66 us
    all_to_all x1, starting transfers between devices, on_device(): gathered = lax.all_to_all(ends, 'seq', 0, 0, tiled=True)  6.47 us
    ppermute x1, starting transfers between devices, on_device(): halo = lax.ppermute(tail, 'seq', [(i, i + 1) for i in range(sections - 1)])  4.01 us
  transfers between devices with their start and end apart: 3, of which 0 were waited for; matrix products, arithmetic and copies ran while one was open for 2% of the time, Pallas kernels for 29%

profile of v2, /device:TPU:1, one launch (start us, length us, event | category | flops | bytes accessed | tf_op | source)
XLA Modules:
  0.0 103.2 jit_solution(13757559705087154068)
XLA Ops:
  0.0 0.7 slice.7
  0.7 0.7 slice.6
  1.4 4.0 %collective-permute-start = (bf16[8,1280]{1,0:T(8,128)(2,1)S(1)}, bf16[8,1280]{1,0:T(8,128)(2,1)S(1)}, u32[]{:S(2)}, u32[]{:S(2)}) collective-permute-start(bf16[8,1280]{1,0:T(8,128)(2,1)S(1)} %pad_maximum_fusion), channel_id=1, source_target_pairs={{0,16},{16,32},{32,48},{48,64},{64,80},{80,96},{96,112},{112,128},... | collective-permute-start | bytes 61448 | tf_op jit(solution)/shard_map/ppermute | solution.py:286
  5.4 1.3 %copy.15.mag_ref = f32[16,1]{1,0:T(8,128)} copy(f32[16,1]{0,1:T(1,128)} %bitcast.9) | data formatting | bytes 128 | tf_op jit(solution)/shard_map/broadcast_in_dim | solution.py:305
  6.8 2.3 %shard_map.118 = (f32[16,32,128]{2,1,0:T(8,128)}, bf16[16,32,128]{2,1,0:T(8,128)(2,1)}, bf16[16,96,128]{2,1,0:T(8,128)(2,1)}, bf16[32,128]{1,0:T(8,128)(2,1)}) custom-call(f32[16,2048]{1,0:T(8,128)} %raw_ref.1, f32[16,1]{1,0:T(8,128)} %copy.15.mag_ref, f32[128,256]{1,0:T(8,128)} %constant.7.clone.tri_ref), custom_call_target="tpu_custom_call" | custom-call | flops 10000000 | bytes 1000000 | tf_op jit(solution)/shard_map/pallas_call | solution.py:295
  9.0 0.0 collective-permute-done.halo_ref
  9.1 0.0 copy-start.2
  9.1 0.6 copy-done.2
  9.7 12.5 %shard_map.119 = (bf16[2048,1024]{1,0:T(8,128)(2,1)}, bf16[2048,256]{1,0:T(8,128)(2,1)}, bf16[16,16,1024]{2,1,0:T(8,128)(2,1)}) custom-call(bf16[2048,1024]{1,0:T(8,128)(2,1)} %feat_ref.1, bf16[2048,256]{1,0:T(8,128)(2,1)} %coup_ref.1, bf16[8,1280]{1,0:T(8,128)(2,1)} %copy-done.2, f32[4,1024]{1,0:T(4,128)} %taps_ref.1, f32[1,1024]{1,0:T(1,128)} %bitcast.7, ...), custom_call_target="tpu_custom_call" | custom-call | flops 1000000000 | bytes 10000000 | tf_op jit(solution)/shard_map/pallas_call | solution.py:308
  22.2 6.5 %all-to-all-start = ((bf16[16,16,1024]{2,1,0:T(8,128)(2,1)}), bf16[16,16,1024]{2,1,0:T(8,128)(2,1)S(1)}, u32[]{:S(2)}, u32[]{:S(2)}) async-start(bf16[16,16,1024]{2,1,0:T(8,128)(2,1)} %get-tuple-element.22), calls=%async_computation | async-start | bytes 1048576 | tf_op jit(solution)/shard_map/all_to_all | solution.py:385
  28.6 0.9 broadcast_in_dim.18.state_ref
  29.5 13.5 %shard_map.120 = (bf16[2048,1024]{1,0:T(8,128)(2,1)}, bf16[2048,1024]{1,0:T(8,128)(2,1)}, f32[128,1024]{1,0:T(8,128)}) custom-call(bf16[2048,1024]{1,0:T(8,128)(2,1)} %get-tuple-element.23.filt_ref, bf16[2048,256]{1,0:T(8,128)(2,1)} %get-tuple-element.21.coupled_ref.read_ref, bf16[2048,1024]{1,0:T(8,128)(2,1)} %gate_ref.3, ...), custom_call_target="tpu_custom_call" | custom-call | flops 2400000000 | bytes 8000000 | tf_op jit(solution)/shard_map/pallas_call | solution.py:354
  43.0 0.0 all-to-all-done.pay_ref
  43.0 0.0 copy-start
  43.0 0.8 copy-done
  43.9 1.9 %shard_map.121.order_ref = bf16[16,8,1024]{2,1,0:T(8,128)(2,1)} custom-call(bf16[16,16,1024]{2,1,0:T(8,128)(2,1)} %copy-done, f32[128,1024]{1,0:T(8,128)} %get-tuple-element.26.order_ref.state_ref), custom_call_target="tpu_custom_call" | custom-call | flops 1000000 | bytes 1000000 | tf_op jit(solution)/shard_map/pallas_call | solution.py:387
  45.7 6.7 %all-to-all-start.1 = ((bf16[16,8,1024]{2,1,0:T(8,128)(2,1)}), bf16[16,8,1024]{2,1,0:T(8,128)(2,1)S(1)}, u32[]{:S(2)}, u32[]{:S(2)}) async-start(bf16[16,8,1024]{2,1,0:T(8,128)(2,1)} %shard_map.121.order_ref), calls=%async_computation.1 | async-start | bytes 524288 | tf_op jit(solution)/shard_map/all_to_all | solution.py:396
  52.4 13.6 %shard_map.122 = (bf16[2048,1024]{1,0:T(8,128)(2,1)}, bf16[2048,1024]{1,0:T(8,128)(2,1)}, f32[128,1024]{1,0:T(8,128)}) custom-call(bf16[2048,1024]{1,0:T(8,128)(2,1)} %get-tuple-element.23.filt_ref, bf16[2048,256]{1,0:T(8,128)(2,1)} %get-tuple-element.21.coupled_ref.read_ref, ...), custom_call_target="tpu_custom_call", output_to_operand_aliasing={{0}: (8, {}), {1}: (9, {})} | custom-call | flops 2400000000 | bytes 8000000 | tf_op jit(solution)/shard_map/pallas_call | solution.py:354
  66.0 0.0 all-to-all-done.1
  66.1 0.0 copy-start.1
  66.1 0.7 copy-done.1
  66.8 9.6 %shard_map.123 = (bf16[2048,1024]{1,0:T(8,128)(2,1)}, f32[16,16,128]{2,1,0:T(8,128)}) custom-call(bf16[2048,256]{1,0:T(8,128)(2,1)} %get-tuple-element.21.coupled_ref.read_ref, bf16[128,1024]{1,0:T(8,128)(2,1)} %bitcast.5, bf16[2048,1024]{1,0:T(8,128)(2,1)} %get-tuple-element.29.yg_ref, bf16[2048,1024]{1,0:T(8,128)(2,1)} %get-tuple-element.30.gp_ref), custom_call_target="tpu_custom_call" | custom-call | flops 600000000 | bytes 12000000 | tf_op jit(solution)/shard_map/pallas_call | solution.py:399
  76.4 19.3 %all_to_all.15.sums_ref = f32[16,16,128]{2,1,0:T(8,128)} all-to-all(f32[16,16,128]{2,1,0:T(8,128)} %get-tuple-element.32), channel_id=1, replica_groups=mesh['seq'=16,'mp'=16] {'mp'}, dimensions={0} | all-to-all | bytes 262144 | tf_op jit(solution)/shard_map/all_to_all | solution.py:420
  95.6 7.6 %shard_map.124 = bf16[2048,1024]{1,0:T(8,128)(2,1)} custom-call(bf16[2048,1024]{1,0:T(8,128)(2,1)} %get-tuple-element.31.gated_ref, f32[16,16,128]{2,1,0:T(8,128)} %all_to_all.15.sums_ref, f32[1,1024]{1,0:T(1,128)} %bitcast.6), custom_call_target="tpu_custom_call" | custom-call | flops 10000000 | bytes 8000000 | tf_op jit(solution)/shard_map/pallas_call | solution.py:422
  (1 shorter events, 0.0 us)
Async XLA Ops:
  1.4 7.6 %collective-permute-start = (bf16[8,1280]{1,0:T(8,128)(2,1)S(1)}, bf16[8,1280]{1,0:T(8,128)(2,1)S(1)}, u32[]{:S(2)}, u32[]{:S(2)}) collective-permute-start(bf16[8,1280]{1,0:T(8,128)(2,1)S(1)} %pad_maximum_fusion), channel_id=1, source_target_pairs={{0,16},{16,32},{32,48},{48,64},{64,80},{80,96},{96,112},{112,128},... | collective-permute-start | bytes 61448 | tf_op jit(solution)/shard_map/ppermute | solution.py:286
  9.1 0.6 copy-start.2
  22.2 20.9 %all-to-all-start = ((bf16[16,16,1024]{2,1,0:T(8,128)(2,1)}), bf16[16,16,1024]{2,1,0:T(8,128)(2,1)S(1)}, u32[]{:S(2)}, u32[]{:S(2)}) async-start(bf16[16,16,1024]{2,1,0:T(8,128)(2,1)} %get-tuple-element.22), calls=%async_computation | async-start | bytes 1048576 | tf_op jit(solution)/shard_map/all_to_all | solution.py:385
  43.0 0.8 copy-start
  45.7 20.3 %all-to-all-start.1 = ((bf16[16,8,1024]{2,1,0:T(8,128)(2,1)}), bf16[16,8,1024]{2,1,0:T(8,128)(2,1)S(1)}, u32[]{:S(2)}, u32[]{:S(2)}) async-start(bf16[16,8,1024]{2,1,0:T(8,128)(2,1)} %shard_map.121.order_ref), calls=%async_computation.1 | async-start | bytes 524288 | tf_op jit(solution)/shard_map/all_to_all | solution.py:396
  66.1 0.7 copy-start.1

commit v3 on v2

v3 whole, which is shorter than its diff:
```python
import functools
import math

import jax
import jax.numpy as jnp
import numpy as np
from jax import lax
from jax.experimental import pallas as pl
from jax.experimental.pallas import tpu as pltpu
from jax.sharding import PartitionSpec as P

CHUNK = 128
LANES = 128
HALO = 8
HEAD_DIM = 64
LOG2E = math.log2(math.e)
BF16 = jnp.bfloat16
F32 = jnp.float32


def params(mib, **flags):
    return pltpu.CompilerParams(vmem_limit_bytes=mib << 20, flags=flags or None)


def far(x):
    return pltpu.with_memory_space_constraint(x, pltpu.HBM)


def cost(flops, nbytes, trans=0):
    return pl.CostEstimate(flops=flops, bytes_accessed=nbytes, transcendentals=trans)


def split(v):
    high = v.astype(BF16)
    return high, (v - high.astype(F32)).astype(BF16)


def contract_rows(a, b):
    return lax.dot_general(a, b, (((0,), (0,)), ((), ())), preferred_element_type=F32)


def contract_lanes(a, b):
    return lax.dot_general(a, b, (((1,), (1,)), ((), ())), preferred_element_type=F32)


def tail_kernel(feat_ref, coup_ref, out_ref):
    channels = feat_ref.shape[1]
    out_ref[:, :channels] = feat_ref[...]
    out_ref[:, channels:] = coup_ref[...]


def decay_kernel(raw_ref, mag_ref, row_ref, wch_ref, ex_ref, run_ref, table_ref):
    heads, tokens = raw_ref.shape
    chunks = tokens // CHUNK
    raw = raw_ref[...]
    small = jnp.exp(-jnp.abs(raw))
    grown = 1.0 + small
    rest = grown - 1.0
    safe = jnp.where(rest == 0.0, 1.0, rest)
    log1p = jnp.where(rest == 0.0, small, jnp.log(grown) * (small / safe))
    step = jnp.maximum(raw, 0.0) + log1p
    diagonal = lax.broadcasted_iota(jnp.int32, (heads, heads), 0) == lax.broadcasted_iota(
        jnp.int32, (heads, heads), 1
    )
    slope = -LOG2E * jnp.sum(jnp.where(diagonal, jnp.exp(mag_ref[...]), 0.0), axis=1, keepdims=True)
    stacked = jnp.concatenate(
        [step[:, c * CHUNK : (c + 1) * CHUNK] for c in range(chunks)], axis=0
    )
    slopes = jnp.concatenate([slope] * chunks, axis=0)
    source = lax.broadcasted_iota(jnp.int32, (CHUNK, 2 * CHUNK), 0)
    target = lax.broadcasted_iota(jnp.int32, (CHUNK, 2 * CHUNK), 1)
    tri = ((target < CHUNK) & (source <= target)) | ((target >= CHUNK) & (source > target - CHUNK))
    sums = jnp.dot(
        stacked * slopes,
        jnp.where(tri, 1.0, 0.0),
        precision=lax.Precision.HIGHEST,
        preferred_element_type=F32,
    )
    lane = lax.broadcasted_iota(jnp.int32, (heads, LANES), 1)
    before = jnp.zeros((heads, 1), F32)
    decays = jnp.zeros((heads, LANES), F32)
    for c in range(chunks):
        rows = slice(c * heads, (c + 1) * heads)
        total = sums[rows, CHUNK - 1 : CHUNK]
        decays = jnp.where(lane == c, total, decays)
        upto = sums[rows, :CHUNK]
        amount = stacked[rows]
        row_ref[c, 0:heads] = upto
        row_ref[c, heads : 2 * heads] = amount
        high, low = split(amount * jnp.exp2(sums[rows, CHUNK:]))
        wch_ref[c, 0:heads] = high
        wch_ref[c, heads : 2 * heads] = low
        high, low = split(jnp.exp2(upto))
        ex_ref[c, 0:heads] = high
        ex_ref[c, heads : 2 * heads] = low
        high, low = split(jnp.exp2(upto + before))
        run_ref[c, 0:heads] = high
        run_ref[c, heads : 2 * heads] = low
        before = before + total
    high, low = split(jnp.exp2(jnp.where(lane == chunks, before, decays)))
    table_ref[0:heads] = high
    table_ref[heads : 2 * heads] = low


def mixed(ext_ref, tile, first, taps, bias):
    start = first + HALO - 3
    half = jnp.broadcast_to(0.5 * bias, (CHUNK, LANES))
    halves = 0.5 * taps
    for k in range(4):
        half = half + halves[k : k + 1] * ext_ref[tile, start + k : start + k + CHUNK, :]
    return half + half * jnp.tanh(half)


def ends_kernel(
    feat_ref, coup_ref, halo_ref, taps_ref, bias_ref, ctaps_ref, cbias_ref, wch_ref, table_ref, spread_ref,
    filt_ref, coupled_ref, states_ref, pay_ref, ext_ref, acc_ref, decay_ref,
):
    i = pl.program_id(0)
    length, channels = feat_ref.shape
    tiles = channels // LANES
    ctiles = coup_ref.shape[1] // LANES
    per = length // CHUNK
    width = 2 * LANES

    @pl.when(i == 0)
    def _():
        for j in range(tiles + ctiles):
            ext_ref[j, 0:HALO, :] = halo_ref[:, j * LANES : (j + 1) * LANES].astype(F32)
        acc_ref[...] = jnp.zeros_like(acc_ref)
        decay_ref[...] = contract_rows(table_ref[...], spread_ref[...])

    @pl.when(i > 0)
    def _():
        for j in range(tiles + ctiles):
            ext_ref[j, 0:HALO, :] = ext_ref[j, length : length + HALO, :]

    for j in range(ctiles):
        part = slice(j * LANES, (j + 1) * LANES)
        ext_ref[tiles + j, HALO : HALO + length, :] = coup_ref[:, part].astype(F32)
    for j in range(tiles):
        part = slice(j * LANES, (j + 1) * LANES)
        ext_ref[j, HALO : HALO + length, :] = feat_ref[:, part].astype(F32)
    for c in range(per):
        rows = slice(c * CHUNK, (c + 1) * CHUNK)
        for j in range(ctiles):
            part = slice(j * LANES, (j + 1) * LANES)
            coupled_ref[rows, part] = mixed(
                ext_ref, tiles + j, c * CHUNK, ctaps_ref[:, part], cbias_ref[:, part]
            ).astype(BF16)
        inputs = coupled_ref[rows, :LANES].T
        columns = wch_ref[c].T
        for q in range(channels // width):
            lanes = slice(q * width, (q + 1) * width)
            scale = jnp.dot(columns, spread_ref[:, lanes], preferred_element_type=F32)
            weighted = []
            for p in range(2):
                j = 2 * q + p
                part = slice(j * LANES, (j + 1) * LANES)
                value = mixed(ext_ref, j, c * CHUNK, taps_ref[:, part], bias_ref[:, part])
                filt_ref[rows, part] = value.astype(BF16)
                weighted.append((value * scale[:, p * LANES : (p + 1) * LANES]).astype(BF16))
            state = acc_ref[:, lanes]
            states_ref[c, :, lanes] = state.astype(BF16)
            decay = decay_ref[pl.ds(i * per + c, 1), lanes]
            acc_ref[:, lanes] = state * decay + jnp.dot(
                inputs, jnp.concatenate(weighted, axis=1), preferred_element_type=F32
            )

    @pl.when(i == pl.num_programs(0) - 1)
    def _():
        final = per * pl.num_programs(0)
        high, low = split(decay_ref[final : final + 1])
        rank = lax.broadcasted_iota(jnp.int32, (8, channels), 0)
        decays = jnp.where(rank == 6, high.astype(F32), low.astype(F32))
        parts = pay_ref.shape[0]
        share = LANES // parts
        for j in range(parts):
            pay_ref[j, 0:share] = acc_ref[j * share : (j + 1) * share].astype(BF16)
            rest = split(acc_ref[j * share : j * share + 8])[1].astype(F32)
            pay_ref[j, share : share + 8] = jnp.where(rank < 6, rest, decays).astype(BF16)


def relay_kernel(pay_ref, order_ref, out_ref):
    parts, rows, channels = pay_ref.shape
    share = rows - 8
    rank = lax.broadcasted_iota(jnp.int32, (8, channels), 0)
    entering = jnp.zeros(out_ref.shape[1:], F32)
    for j in range(parts):
        out_ref[j] = entering
        tail = pay_ref[j, share : share + 8].astype(F32)
        decay = tail[6:7] + tail[7:8]
        ends = pay_ref[j, 0:8].astype(F32) + jnp.where(rank < 6, tail, 0.0)
        if share > 8:
            ends = jnp.concatenate([ends, pay_ref[j, 8:share].astype(F32)], axis=0)
        entering = decay * entering + ends


def inside_kernel(filt_ref, coupled_ref, row_ref, ex_ref, states_ref, spread_ref, order_ref, *rest):
    out_ref = rest[-1]
    heads = row_ref.shape[1] // 2
    length, channels = filt_ref.shape
    above = lax.broadcasted_iota(jnp.int32, (CHUNK, CHUNK), 0)
    below = lax.broadcasted_iota(jnp.int32, (CHUNK, CHUNK), 1)
    lane = lax.broadcasted_iota(jnp.int32, (CHUNK, LANES), 1)
    left = lane < HEAD_DIM
    width = 2 * LANES
    chunks = []
    for c in range(length // CHUNK):
        rows = slice(c * CHUNK, (c + 1) * CHUNK)
        reads = coupled_ref[rows, LANES:]
        scores = jnp.where(above >= below, contract_lanes(reads, coupled_ref[rows, :LANES]), 0.0)
        chunks.append((c, rows, reads, scores, row_ref[c, 0:heads].T, ex_ref[c].T))

    def part(q, c, rows, reads, scores, columns, decays):
        lanes = slice(q * width, (q + 1) * width)
        decayed = jnp.dot(decays, spread_ref[:, lanes], preferred_element_type=F32)
        carried = jnp.dot(reads, states_ref[c, :, lanes], preferred_element_type=F32) * decayed
        for p in range(2):
            weights = []
            for h in (4 * q + 2 * p, 4 * q + 2 * p + 1):
                gap = jnp.minimum(columns[:, h : h + 1] - row_ref[c, h : h + 1], 0.0)
                amount = row_ref[c, heads + h : heads + h + 1]
                weights.append((jnp.exp2(gap) * scores * amount).astype(BF16))
            start = q * width + p * LANES
            pair = filt_ref[rows, start : start + LANES]
            inside = jnp.dot(jnp.concatenate(weights, axis=0), pair, preferred_element_type=F32)
            inside = jnp.where(left, inside[:CHUNK], inside[CHUNK:])
            out_ref[rows, start : start + LANES] = (
                carried[:, p * LANES : (p + 1) * LANES] + inside
            ).astype(BF16)

    for q in range(channels // width):
        for held in chunks:
            part(q, *held)


def gated_kernel(
    read_ref, enter_ref, value_ref, gate_ref, run_ref, spread_ref, gain_ref, gated_ref, out_ref, sums_ref,
    parts_ref,
):
    i = pl.program_id(0)

    @pl.when(i == 0)
    def _():
        high, low = split(enter_ref[...])
        parts_ref[0:LANES] = high
        parts_ref[LANES : 2 * LANES] = low

    length, channels = value_ref.shape
    per = length // CHUNK
    columns = jnp.concatenate([run_ref[c].T for c in range(per)], axis=0)
    reads = jnp.concatenate([read_ref[...], read_ref[...]], axis=1)
    rows = slice(0, length)
    squares = jnp.zeros((length, LANES), F32)
    width = 2 * LANES
    for q in range(channels // width):
        lanes = slice(q * width, (q + 1) * width)
        running = jnp.dot(columns, spread_ref[:, lanes], preferred_element_type=F32)
        before = jnp.dot(reads, parts_ref[:, lanes], preferred_element_type=F32)
        half = (gate_ref[rows, lanes] * 0.5).astype(F32)
        opened = half + half * jnp.tanh(half)
        gated = (value_ref[rows, lanes].astype(F32) + running * before) * opened
        gated_ref[rows, lanes] = (gated * gain_ref[:, lanes]).astype(BF16)
        squares = squares + gated[:, :LANES] * gated[:, :LANES]
        squares = squares + gated[:, LANES:] * gated[:, LANES:]
    totals = contract_lanes(jnp.ones((8, LANES), BF16), squares.astype(BF16))
    for c in range(per):
        sums_ref[pl.ds(i * per + c, 1), :] = totals[0:1, c * CHUNK : (c + 1) * CHUNK]

    @pl.when(i == pl.num_programs(0) - 1)
    def _():
        mine = sums_ref[...].astype(out_ref.dtype)
        for j in range(out_ref.shape[0]):
            out_ref[j] = mine


def normal_kernel(inner, gated_ref, sums_ref, out_ref, scale_ref):
    i = pl.program_id(0)
    length, channels = gated_ref.shape
    chunks = sums_ref.shape[1]

    @pl.when(i == 0)
    def _():
        total = sums_ref[0].astype(F32)
        for j in range(1, sums_ref.shape[0]):
            total = total + sums_ref[j].astype(F32)
        columns = lax.rsqrt(total / inner + 1e-05).T
        for c in range(chunks):
            scale_ref[c] = jnp.broadcast_to(columns[:, c : c + 1], (CHUNK, LANES))

    per = length // CHUNK
    for c in range(per):
        rows = slice(c * CHUNK, (c + 1) * CHUNK)
        scale = scale_ref[i * per + c]
        for j in range(channels // LANES):
            lanes = slice(j * LANES, (j + 1) * LANES)
            out_ref[rows, lanes] = (gated_ref[rows, lanes].astype(F32) * scale).astype(BF16)


def whole(shape):
    return pl.BlockSpec(shape, lambda i: (0,) * len(shape))


def on_device(
    features,
    coupling,
    gate_values,
    step_raw,
    decay_log,
    feature_taps,
    feature_offset,
    coupling_taps,
    coupling_offset,
    norm_gain,
):
    tokens, channels = features.shape
    heads = decay_log.shape[0]
    sections = lax.axis_size("seq")
    groups = lax.axis_size("mp")
    chunks = tokens // CHUNK
    share = LANES // sections
    any_spec = pl.BlockSpec(memory_space=pl.ANY)

    block = 2 * CHUNK
    tail = pl.pallas_call(
        tail_kernel,
        grid=(1,),
        in_specs=[
            pl.BlockSpec((HALO, channels), lambda i: (tokens // HALO - 1, 0)),
            pl.BlockSpec((HALO, 2 * LANES), lambda i: (tokens // HALO - 1, 0)),
        ],
        out_specs=whole((HALO, channels + 2 * LANES)),
        out_shape=pltpu.VMEM((HALO, channels + 2 * LANES), BF16),
        compiler_params=params(4),
        cost_estimate=cost(10**4, 5 * 10**4),
    )(far(features), far(coupling))
    halo = lax.ppermute(tail, "seq", [(i, i + 1) for i in range(sections - 1)])

    one = np.arange(channels)[None, :] // HEAD_DIM == np.arange(heads)[:, None]
    spread = jnp.asarray(np.concatenate([one, one], axis=0), BF16)

    rows, wch, ex, run, table = pl.pallas_call(
        decay_kernel,
        grid=(1,),
        in_specs=[whole((heads, tokens)), whole((1, heads))],
        out_specs=(
            whole((chunks, 2 * heads, CHUNK)),
            whole((chunks, 2 * heads, CHUNK)),
            whole((chunks, 2 * heads, CHUNK)),
            whole((chunks, 2 * heads, CHUNK)),
            whole((2 * heads, LANES)),
        ),
        out_shape=(
            pltpu.VMEM((chunks, 2 * heads, CHUNK), F32),
            pltpu.VMEM((chunks, 2 * heads, CHUNK), BF16),
            pltpu.VMEM((chunks, 2 * heads, CHUNK), BF16),
            pltpu.VMEM((chunks, 2 * heads, CHUNK), BF16),
            pltpu.VMEM((2 * heads, LANES), BF16),
        ),
        compiler_params=params(8),
        cost_estimate=cost(10**7, 10**6, 10**5),
    )(far(step_raw), decay_log[None, :])

    filtered, coupled, states, ends = pl.pallas_call(
        ends_kernel,
        grid=(tokens // block,),
        in_specs=[
            pl.BlockSpec((block, channels), lambda i: (i, 0)),
            pl.BlockSpec((block, 2 * LANES), lambda i: (i, 0)),
            whole((HALO, channels + 2 * LANES)),
            whole((4, channels)),
            whole((1, channels)),
            whole((4, 2 * LANES)),
            whole((1, 2 * LANES)),
            pl.BlockSpec((2, 2 * heads, CHUNK), lambda i: (i, 0, 0)),
            whole((2 * heads, LANES)),
            whole((2 * heads, channels)),
        ],
        out_specs=(
            pl.BlockSpec((block, channels), lambda i: (i, 0)),
            pl.BlockSpec((block, 2 * LANES), lambda i: (i, 0)),
            pl.BlockSpec((2, LANES, channels), lambda i: (i, 0, 0)),
            whole((sections, share + 8, channels)),
        ),
        out_shape=(
            pltpu.HBM((tokens, channels), BF16),
            pltpu.HBM((tokens, 2 * LANES), BF16),
            pltpu.HBM((chunks, LANES, channels), BF16),
            jax.ShapeDtypeStruct((sections, share + 8, channels), BF16),
        ),
        scratch_shapes=[
            pltpu.VMEM((channels // LANES + 2, HALO + block, LANES), F32),
            pltpu.VMEM((LANES, channels), F32),
            pltpu.VMEM((LANES, channels), F32),
        ],
        compiler_params=params(24),
        cost_estimate=cost(10**9, 10**7, 2 * 10**6),
    )(
        far(features),
        far(coupling),
        halo,
        far(feature_taps),
        far(feature_offset[None, :]),
        far(coupling_taps),
        far(coupling_offset[None, :]),
        wch,
        table,
        far(spread),
    )

    def inside(first, count, order, *held):
        return pl.pallas_call(
            inside_kernel,
            grid=(count,),
            in_specs=[
                pl.BlockSpec((block, channels), lambda i: (first + i, 0)),
                pl.BlockSpec((block, 2 * LANES), lambda i: (first + i, 0)),
                pl.BlockSpec((2, 2 * heads, CHUNK), lambda i: (first + i, 0, 0)),
                pl.BlockSpec((2, 2 * heads, CHUNK), lambda i: (first + i, 0, 0)),
                pl.BlockSpec((2, LANES, channels), lambda i: (first + i, 0, 0)),
                whole((2 * heads, channels)),
                any_spec,
            ]
            + [any_spec] * len(held),
            out_specs=pl.BlockSpec((block, channels), lambda i: (first + i, 0)),
            out_shape=pltpu.HBM((tokens, channels), BF16),
            input_output_aliases={7 + k: k for k in range(len(held))},
            compiler_params=params(24),
            cost_estimate=cost(count * 6 * 10**8, count * 2 * 10**6, count * 6 * 10**5),
        )(far(filtered), far(coupled), rows, ex, far(states), far(spread), order, *held)

    steps = tokens // block
    half = steps // 2
    gathered = lax.all_to_all(ends, "seq", 0, 0, tiled=True)
    value = inside(0, half, table)
    starts = pl.pallas_call(
        relay_kernel,
        grid=(1,),
        in_specs=[whole((sections, share + 8, channels)), any_spec],
        out_specs=whole((sections, share, channels)),
        out_shape=jax.ShapeDtypeStruct((sections, share, channels), F32),
        compiler_params=params(8),
        cost_estimate=cost(10**6, 10**6),
    )(gathered, far(value))
    entering = lax.all_to_all(starts, "seq", 0, 0, tiled=True).reshape(LANES, channels)
    value = inside(half, steps - half, starts, far(value))
    gated, squares = pl.pallas_call(
        gated_kernel,
        grid=(tokens // block,),
        in_specs=[
            pl.BlockSpec((block, LANES), lambda i: (i, 1)),
            whole((LANES, channels)),
            pl.BlockSpec((block, channels), lambda i: (i, 0)),
            pl.BlockSpec((block, channels), lambda i: (i, 0)),
            pl.BlockSpec((2, 2 * heads, CHUNK), lambda i: (i, 0, 0)),
            whole((2 * heads, channels)),
            whole((1, channels)),
        ],
        out_specs=(
            pl.BlockSpec((block, channels), lambda i: (i, 0)),
            whole((groups, chunks, CHUNK)),
        ),
        out_shape=(
            pltpu.VMEM((tokens, channels), BF16),
            jax.ShapeDtypeStruct((groups, chunks, CHUNK), BF16),
        ),
        scratch_shapes=[
            pltpu.VMEM((chunks, CHUNK), F32),
            pltpu.VMEM((2 * LANES, channels), BF16),
        ],
        compiler_params=params(16),
        cost_estimate=cost(6 * 10**8, 12 * 10**6),
    )(
        far(coupled), entering, far(value), far(gate_values), run, far(spread), far(norm_gain[None, :])
    )
    squares = lax.all_to_all(squares, "mp", 0, 0, tiled=True)

    return pl.pallas_call(
        functools.partial(normal_kernel, float(channels * groups)),
        grid=(tokens // block,),
        in_specs=[
            pl.BlockSpec((block, channels), lambda i: (i, 0)),
            whole((groups, chunks, CHUNK)),
        ],
        out_specs=pl.BlockSpec((block, channels), lambda i: (i, 0)),
        out_shape=jax.ShapeDtypeStruct((tokens, channels), BF16),
        scratch_shapes=[pltpu.VMEM((chunks, CHUNK, LANES), F32)],
        compiler_params=params(16),
        cost_estimate=cost(10**7, 8 * 10**6),
    )(gated, squares)


def solution(mesh):
    in_specs = (
        P("seq", "mp"),
        P("seq", None),
        P("seq", "mp"),
        P("mp", "seq"),
        P("mp"),
        P(None, "mp"),
        P("mp"),
        P(),
        P(),
        P("mp"),
    )
    out_specs = P("seq", "mp")
    return jax.shard_map(
        on_device, mesh=mesh, in_specs=in_specs, out_specs=out_specs, check_vma=False
    )
```

time: 104 us -> 83 us (0.80)
  Pallas kernels: 61 us -> 42.8 us
  local copies, waits for them, and re-layouts: 5.72 us -> 0.01 us
  waiting for transfers between devices: 0.01 us -> 4.77 us
  starting transfers between devices: 17.1 us -> 14.8 us
    pallas_call x3 -> x4, Pallas kernels: 29.4 us -> 15.8 us  [the longest x2 13.6 us: inside(): pl.pallas_call(inside_kernel, grid=(count,), in_specs=[pl.BlockSpec((bloc...]
    pallas_call x1, Pallas kernels: 7.57 us -> 4.36 us  [on_device(): pl.pallas_call(functools.partial(normal_kernel, float(channels * groups))...]
    all_to_all x1, starting transfers between devices: 6.66 us -> 4.21 us  [on_device(): lax.all_to_all(starts, 'seq', 0, 0, tiled=True).reshape(LANES, channels)]
    all_to_all x1, waiting for transfers between devices: 0.01 us -> 2.44 us  [on_device(): gathered = lax.all_to_all(ends, 'seq', 0, 0, tiled=True)]
    all_to_all x1, waiting for transfers between devices: 0.01 us -> 2.32 us  [on_device(): lax.all_to_all(starts, 'seq', 0, 0, tiled=True).reshape(LANES, channels)]
    broadcast_in_dim x2 -> x0, local copies, waits for them, and re-layouts: 2.2 us -> none  [the longest x1 1.33 us: on_device(): decay_log[:, None]]
    unnamed x6 -> x2, local copies, waits for them, and re-layouts: 2.12 us -> 0.01 us
    slice x2 -> x0, local copies, waits for them, and re-layouts: 1.41 us -> none  [the longest x1 0.72 us: on_device(): features[tokens - HALO:]]
  transfers between devices with their start and end apart: 3 -> 3, of which waited for: 0 -> 2; matrix products, arithmetic and copies ran while one was open for 2% -> 0% of each run, Pallas kernels for 29% -> 18%
where the time goes in v3:
time: 83 us; the launch traced here: 82.1 us
  Pallas kernels  42.8 us (52%)
  blocking collectives  19.7 us (24%)
  starting transfers between devices  14.8 us (18%)
  waiting for transfers between devices  4.77 us (6%)
    all_to_all x1, blocking collectives, on_device(): squares = lax.all_to_all(squares, 'mp', 0, 0, tiled=True)  19.7 us
    pallas_call x2, Pallas kernels, inside(): pl.pallas_call(inside_kernel, grid=(count,), in_specs=[pl.BlockSpec((bloc...  13.6 us
    pallas_call x1, Pallas kernels, on_device(): pl.pallas_call(ends_kernel, grid=(tokens // block,), in_specs=[pl.BlockSp...  12.9 us
    pallas_call x1, Pallas kernels, on_device(): pl.pallas_call(gated_kernel, grid=(tokens // block,), in_specs=[pl.BlockS...  8.79 us
    all_to_all x1, starting transfers between devices, on_device(): gathered = lax.all_to_all(ends, 'seq', 0, 0, tiled=True)  6.55 us
    pallas_call x1, Pallas kernels, on_device(): pl.pallas_call(functools.partial(normal_kernel, float(channels * groups))...  4.36 us
    all_to_all x1, starting transfers between devices, on_device(): lax.all_to_all(starts, 'seq', 0, 0, tiled=True).reshape(LANES, channels)  4.21 us
    ppermute x1, starting transfers between devices, on_device(): halo = lax.ppermute(tail, 'seq', [(i, i + 1) for i in range(sections - 1)])  4.01 us
  transfers between devices with their start and end apart: 3, of which 2 were waited for; matrix products, arithmetic and copies ran while one was open for 0% of the time, Pallas kernels for 18%

profile of v3, /device:TPU:1, one launch (start us, length us, event | category | flops | bytes accessed | tf_op | source)
XLA Modules:
  0.0 82.1 jit_solution(12533295823992397209)
XLA Ops:
  0.0 0.0 copy-start
  0.0 0.7 shard_map.109
  0.7 4.0 %collective-permute-start = (bf16[8,1280]{1,0:T(8,128)(2,1)S(1)}, bf16[8,1280]{1,0:T(8,128)(2,1)S(1)}, u32[]{:S(2)}, u32[]{:S(2)}) collective-permute-start(bf16[8,1280]{1,0:T(8,128)(2,1)S(1)} %shard_map.109), channel_id=1, source_target_pairs={{0,16},{16,32},{32,48},{48,64},{64,80},{80,96},{96,112},{112,128},... | collective-permute-start | bytes 61448 | tf_op jit(solution)/shard_map/ppermute | solution.py:337
  4.8 0.0 copy-done
  4.8 1.5 %shard_map.110 = (f32[16,32,128]{2,1,0:T(8,128)S(1)}, bf16[16,32,128]{2,1,0:T(8,128)(2,1)S(1)}, bf16[16,32,128]{2,1,0:T(8,128)(2,1)S(1)}, bf16[16,32,128]{2,1,0:T(8,128)(2,1)S(1)}, bf16[32,128]{1,0:T(8,128)(2,1)S(1)}) custom-call(f32[16,2048]{1,0:T(8,128)} %raw_ref.1, f32[1,16]{1,0:T(1,128)S(1)} %bitcast.6), custom_call_target="tpu_custom_call" | custom-call | flops 10000000 | bytes 1000000 | tf_op jit(solution)/shard_map/pallas_call | solution.py:342
  6.3 0.0 collective-permute-done.halo_ref
  6.3 12.9 %shard_map.111 = (bf16[2048,1024]{1,0:T(8,128)(2,1)}, bf16[2048,256]{1,0:T(8,128)(2,1)}, bf16[16,128,1024]{2,1,0:T(8,128)(2,1)}, bf16[16,16,1024]{2,1,0:T(8,128)(2,1)}) custom-call(bf16[2048,1024]{1,0:T(8,128)(2,1)} %feat_ref.3, bf16[2048,256]{1,0:T(8,128)(2,1)} %coup_ref.3, bf16[8,1280]{1,0:T(8,128)(2,1)S(1)} %collective-permute-done.halo_ref, ...), custom_call_target="tpu_custom_call" | custom-call | flops 1000000000 | bytes 10000000 | tf_op jit(solution)/shard_map/pallas_call | solution.py:364
  19.2 6.5 %all-to-all-start = ((bf16[16,16,1024]{2,1,0:T(8,128)(2,1)}), bf16[16,16,1024]{2,1,0:T(8,128)(2,1)S(1)}, u32[]{:S(2)}, u32[]{:S(2)}) async-start(bf16[16,16,1024]{2,1,0:T(8,128)(2,1)} %get-tuple-element.19), calls=%async_computation | async-start | bytes 1048576 | tf_op jit(solution)/shard_map/all_to_all | solution.py:434
  25.7 6.8 %shard_map.112.order_ref.rest_0_ = bf16[2048,1024]{1,0:T(8,128)(2,1)} custom-call(bf16[2048,1024]{1,0:T(8,128)(2,1)} %get-tuple-element.20.filt_ref, bf16[2048,256]{1,0:T(8,128)(2,1)} %get-tuple-element.18.coupled_ref.read_ref, f32[16,32,128]{2,1,0:T(8,128)S(1)} %get-tuple-element.21.row_ref, bf16[16,32,128]{2,1,0:T(8,128)(2,1)S(1)} %get-tuple-element.22.ex_ref, ...), custom_call_target="tpu_custom_call" | custom-call | flops 2400000000 | bytes 8000000 | tf_op jit(solution)/shard_map/pallas_call | solution.py:412
  32.5 2.4 %all-to-all-done.pay_ref = bf16[16,16,1024]{2,1,0:T(8,128)(2,1)S(1)} async-done(((bf16[16,16,1024]{2,1,0:T(8,128)(2,1)}), bf16[16,16,1024]{2,1,0:T(8,128)(2,1)S(1)}, u32[]{:S(2)}, u32[]{:S(2)}) %all-to-all-start) | async-done | bytes 524320 | tf_op jit(solution)/shard_map/all_to_all | solution.py:434
  34.9 0.9 %shard_map.113.order_ref = f32[16,8,1024]{2,1,0:T(8,128)} custom-call(bf16[16,16,1024]{2,1,0:T(8,128)(2,1)S(1)} %all-to-all-done.pay_ref, bf16[2048,1024]{1,0:T(8,128)(2,1)} %shard_map.112.order_ref.rest_0_), custom_call_target="tpu_custom_call" | custom-call | flops 1000000 | bytes 1000000 | tf_op jit(solution)/shard_map/pallas_call | solution.py:436
  35.9 4.2 %all-to-all-start.1 = ((f32[16,8,1024]{2,1,0:T(8,128)}), f32[16,8,1024]{2,1,0:T(8,128)S(1)}, u32[]{:S(2)}, u32[]{:S(2)}) async-start(f32[16,8,1024]{2,1,0:T(8,128)} %shard_map.113.order_ref), calls=%async_computation.1 | async-start | bytes 1048576 | tf_op jit(solution)/shard_map/all_to_all | solution.py:445
  40.1 6.8 %shard_map.114.value_ref = bf16[2048,1024]{1,0:T(8,128)(2,1)} custom-call(bf16[2048,1024]{1,0:T(8,128)(2,1)} %get-tuple-element.20.filt_ref, bf16[2048,256]{1,0:T(8,128)(2,1)} %get-tuple-element.18.coupled_ref.read_ref, f32[16,32,128]{2,1,0:T(8,128)S(1)} %get-tuple-element.21.row_ref, ...), custom_call_target="tpu_custom_call", output_to_operand_aliasing={{}: (7, {})} | custom-call | flops 2400000000 | bytes 8000000 | tf_op jit(solution)/shard_map/pallas_call | solution.py:412
  46.9 2.3 %all-to-all-done.1 = f32[16,8,1024]{2,1,0:T(8,128)S(1)} async-done(((f32[16,8,1024]{2,1,0:T(8,128)}), f32[16,8,1024]{2,1,0:T(8,128)S(1)}, u32[]{:S(2)}, u32[]{:S(2)}) %all-to-all-start.1) | async-done | bytes 524320 | tf_op jit(solution)/shard_map/all_to_all | solution.py:445
  49.2 8.8 %shard_map.115 = (bf16[2048,1024]{1,0:T(8,128)(2,1)S(1)}, bf16[16,16,128]{2,1,0:T(8,128)(2,1)S(1)}) custom-call(bf16[2048,256]{1,0:T(8,128)(2,1)} %get-tuple-element.18.coupled_ref.read_ref, f32[128,1024]{1,0:T(8,128)S(1)} %bitcast.5, bf16[2048,1024]{1,0:T(8,128)(2,1)} %shard_map.114.value_ref, bf16[2048,1024]{1,0:T(8,128)(2,1)} %gate_ref.1, ...), custom_call_target="tpu_custom_call" | custom-call | flops 600000000 | bytes 12000000 | tf_op jit(solution)/shard_map/pallas_call | solution.py:447
  58.0 19.7 %all_to_all.15.sums_ref = bf16[16,16,128]{2,1,0:T(8,128)(2,1)S(1)} all-to-all(bf16[16,16,128]{2,1,0:T(8,128)(2,1)S(1)} %get-tuple-element.26), channel_id=1, replica_groups=mesh['seq'=16,'mp'=16] {'mp'}, dimensions={0} | all-to-all | bytes 131072 | tf_op jit(solution)/shard_map/all_to_all | solution.py:476
  77.7 4.4 %shard_map.116 = bf16[2048,1024]{1,0:T(8,128)(2,1)} custom-call(bf16[2048,1024]{1,0:T(8,128)(2,1)S(1)} %get-tuple-element.25.gated_ref, bf16[16,16,128]{2,1,0:T(8,128)(2,1)S(1)} %all_to_all.15.sums_ref), custom_call_target="tpu_custom_call" | custom-call | flops 10000000 | bytes 8000000 | tf_op jit(solution)/shard_map/pallas_call | solution.py:478
Async XLA Ops:
  0.0 4.8 %copy-start = (f32[16]{0:T(128)S(1)}, f32[16]{0:T(128)}, u32[]{:S(2)}) copy-start(f32[16]{0:T(128)} %param.15) | copy-start | bytes 196
  0.7 5.5 %collective-permute-start = (bf16[8,1280]{1,0:T(8,128)(2,1)S(1)}, bf16[8,1280]{1,0:T(8,128)(2,1)S(1)}, u32[]{:S(2)}, u32[]{:S(2)}) collective-permute-start(bf16[8,1280]{1,0:T(8,128)(2,1)S(1)} %shard_map.109), channel_id=1, source_target_pairs={{0,16},{16,32},{32,48},{48,64},{64,80},{80,96},{96,112},{112,128},... | collective-permute-start | bytes 61448 | tf_op jit(solution)/shard_map/ppermute | solution.py:337
  19.2 15.7 %all-to-all-start = ((bf16[16,16,1024]{2,1,0:T(8,128)(2,1)}), bf16[16,16,1024]{2,1,0:T(8,128)(2,1)S(1)}, u32[]{:S(2)}, u32[]{:S(2)}) async-start(bf16[16,16,1024]{2,1,0:T(8,128)(2,1)} %get-tuple-element.19), calls=%async_computation | async-start | bytes 1048576 | tf_op jit(solution)/shard_map/all_to_all | solution.py:434
  35.9 13.4 %all-to-all-start.1 = ((f32[16,8,1024]{2,1,0:T(8,128)}), f32[16,8,1024]{2,1,0:T(8,128)S(1)}, u32[]{:S(2)}, u32[]{:S(2)}) async-start(f32[16,8,1024]{2,1,0:T(8,128)} %shard_map.113.order_ref), calls=%async_computation.1 | async-start | bytes 1048576 | tf_op jit(solution)/shard_map/all_to_all | solution.py:445

commit v4 on v3

--- a/solution.py
+++ b/solution.py
@@ -235,66 +235,94 @@
 
 
 def gated_kernel(
-    read_ref, enter_ref, value_ref, gate_ref, run_ref, spread_ref, gain_ref, gated_ref, out_ref, sums_ref,
-    parts_ref,
+    coupled_ref, value_ref, gate_ref, enter_ref, run_ref, spread_ref, gated_ref, out_ref,
+    read_buf, value_buf, gate_buf, sums_ref, parts_ref, read_sem, value_sem, gate_sem,
 ):
-    i = pl.program_id(0)
-
-    @pl.when(i == 0)
-    def _():
-        high, low = split(enter_ref[...])
-        parts_ref[0:LANES] = high
-        parts_ref[LANES : 2 * LANES] = low
-
-    length, channels = value_ref.shape
+    steps, length, channels = value_buf.shape
     per = length // CHUNK
-    columns = jnp.concatenate([run_ref[c].T for c in range(per)], axis=0)
-    reads = jnp.concatenate([read_ref[...], read_ref[...]], axis=1)
-    rows = slice(0, length)
-    squares = jnp.zeros((length, LANES), F32)
     width = 2 * LANES
-    for q in range(channels // width):
-        lanes = slice(q * width, (q + 1) * width)
-        running = jnp.dot(columns, spread_ref[:, lanes], preferred_element_type=F32)
-        before = jnp.dot(reads, parts_ref[:, lanes], preferred_element_type=F32)
-        half = (gate_ref[rows, lanes] * 0.5).astype(F32)
-        opened = half + half * jnp.tanh(half)
-        gated = (value_ref[rows, lanes].astype(F32) + running * before) * opened
-        gated_ref[rows, lanes] = (gated * gain_ref[:, lanes]).astype(BF16)
-        squares = squares + gated[:, :LANES] * gated[:, :LANES]
-        squares = squares + gated[:, LANES:] * gated[:, LANES:]
-    totals = contract_lanes(jnp.ones((8, LANES), BF16), squares.astype(BF16))
-    for c in range(per):
-        sums_ref[pl.ds(i * per + c, 1), :] = totals[0:1, c * CHUNK : (c + 1) * CHUNK]
-
-    @pl.when(i == pl.num_programs(0) - 1)
-    def _():
-        mine = sums_ref[...].astype(out_ref.dtype)
-        for j in range(out_ref.shape[0]):
-            out_ref[j] = mine
-
-
-def normal_kernel(inner, gated_ref, sums_ref, out_ref, scale_ref):
-    i = pl.program_id(0)
-    length, channels = gated_ref.shape
-    chunks = sums_ref.shape[1]
-
-    @pl.when(i == 0)
-    def _():
-        total = sums_ref[0].astype(F32)
-        for j in range(1, sums_ref.shape[0]):
-            total = total + sums_ref[j].astype(F32)
-        columns = lax.rsqrt(total / inner + 1e-05).T
-        for c in range(chunks):
-            scale_ref[c] = jnp.broadcast_to(columns[:, c : c + 1], (CHUNK, LANES))
-
+    reading = pltpu.make_async_copy(coupled_ref.at[:, LANES : 2 * LANES], read_buf, read_sem)
+
+    def arriving(k):
+        rows = pl.ds(pl.multiple_of(k * length, length), length)
+        return (
+            pltpu.make_async_copy(value_ref.at[rows], value_buf.at[k], value_sem.at[k]),
+            pltpu.make_async_copy(gate_ref.at[rows], gate_buf.at[k], gate_sem.at[k]),
+        )
+
+    for k in range(steps):
+        for copy in arriving(k):
+            copy.start()
+        if k == 0:
+            reading.start()
+    high, low = split(enter_ref[...])
+    parts_ref[0:LANES] = high
+    parts_ref[LANES : 2 * LANES] = low
+    reading.wait()
+
+    def step(i, carry):
+        for copy in arriving(i):
+            copy.wait()
+        rows = pl.ds(pl.multiple_of(i * length, length), length)
+        columns = jnp.concatenate([run_ref[i * per + c].T for c in range(per)], axis=0)
+        reads = read_buf[rows]
+        reads = jnp.concatenate([reads, reads], axis=1)
+        squares = jnp.zeros((length, LANES), F32)
+        for q in range(channels // width):
+            lanes = slice(q * width, (q + 1) * width)
+            running = jnp.dot(columns, spread_ref[:, lanes], preferred_element_type=F32)
+            before = jnp.dot(reads, parts_ref[:, lanes], preferred_element_type=F32)
+            half = (gate_buf[i, :, lanes] * 0.5).astype(F32)
+            opened = half + half * jnp.tanh(half)
+            gated = (value_buf[i, :, lanes].astype(F32) + running * before) * opened
+            gated_ref[rows, lanes] = gated.astype(BF16)
+            squares = squares + gated[:, :LANES] * gated[:, :LANES]
+            squares = squares + gated[:, LANES:] * gated[:, LANES:]
+        totals = contract_lanes(jnp.ones((8, LANES), BF16), squares.astype(BF16))
+        for c in range(per):
+            sums_ref[pl.ds(i * per + c, 1), :] = totals[0:1, c * CHUNK : (c + 1) * CHUNK]
+        return carry
+
+    lax.fori_loop(0, steps, step, 0)
+    mine = sums_ref[...].astype(out_ref.dtype)
+    for j in range(out_ref.shape[0]):
+        out_ref[j] = mine
+
+
+def normal_kernel(inner, gated_ref, sums_ref, gain_ref, out_ref, scale_ref, out_buf, out_sem):
+    slots, length, channels = out_buf.shape
+    steps = gated_ref.shape[0] // length
     per = length // CHUNK
-    for c in range(per):
-        rows = slice(c * CHUNK, (c + 1) * CHUNK)
-        scale = scale_ref[i * per + c]
-        for j in range(channels // LANES):
-            lanes = slice(j * LANES, (j + 1) * LANES)
-            out_ref[rows, lanes] = (gated_ref[rows, lanes].astype(F32) * scale).astype(BF16)
+    total = sums_ref[0].astype(F32)
+    for j in range(1, sums_ref.shape[0]):
+        total = total + sums_ref[j].astype(F32)
+    scale_ref[...] = lax.rsqrt(total / inner + 1e-05)
+
+    def leaving(k, slot):
+        rows = pl.ds(pl.multiple_of(k * length, length), length)
+        return pltpu.make_async_copy(out_buf.at[slot], out_ref.at[rows], out_sem.at[slot])
+
+    def step(i, carry):
+        slot = lax.rem(i, slots)
+
+        @pl.when(i >= slots)
+        def _():
+            leaving(i - slots, slot).wait()
+
+        for c in range(per):
+            first = pl.multiple_of(i * length + c * CHUNK, CHUNK)
+            scale = jnp.broadcast_to(scale_ref[pl.ds(i * per + c, 1), :], (CHUNK, LANES)).T
+            for j in range(channels // LANES):
+                lanes = slice(j * LANES, (j + 1) * LANES)
+                out_buf[slot, c * CHUNK : (c + 1) * CHUNK, lanes] = (
+                    gated_ref[pl.ds(first, CHUNK), lanes].astype(F32) * gain_ref[:, lanes] * scale
+                ).astype(BF16)
+        leaving(i, slot).start()
+        return carry
+
+    lax.fori_loop(0, steps, step, 0)
+    for k in range(steps - slots, steps):
+        leaving(k, k % slots).wait()
 
 
 def whole(shape):
@@ -444,50 +472,44 @@
     )(gathered, far(value))
     entering = lax.all_to_all(starts, "seq", 0, 0, tiled=True).reshape(LANES, channels)
     value = inside(half, steps - half, starts, far(value))
+    near_spec = pl.BlockSpec(memory_space=pltpu.VMEM)
     gated, squares = pl.pallas_call(
         gated_kernel,
-        grid=(tokens // block,),
-        in_specs=[
-            pl.BlockSpec((block, LANES), lambda i: (i, 1)),
-            whole((LANES, channels)),
-            pl.BlockSpec((block, channels), lambda i: (i, 0)),
-            pl.BlockSpec((block, channels), lambda i: (i, 0)),
-            pl.BlockSpec((2, 2 * heads, CHUNK), lambda i: (i, 0, 0)),
-            whole((2 * heads, channels)),
-            whole((1, channels)),
-        ],
-        out_specs=(
-            pl.BlockSpec((block, channels), lambda i: (i, 0)),
-            whole((groups, chunks, CHUNK)),
-        ),
+        in_specs=[any_spec] * 3 + [near_spec] * 3,
+        out_specs=(near_spec, near_spec),
         out_shape=(
             pltpu.VMEM((tokens, channels), BF16),
-            jax.ShapeDtypeStruct((groups, chunks, CHUNK), BF16),
+            pltpu.VMEM((groups, chunks, CHUNK), BF16),
         ),
         scratch_shapes=[
+            pltpu.VMEM((tokens, LANES), BF16),
+            pltpu.VMEM((tokens // block, block, channels), BF16),
+            pltpu.VMEM((tokens // block, block, channels), BF16),
             pltpu.VMEM((chunks, CHUNK), F32),
             pltpu.VMEM((2 * LANES, channels), BF16),
+            pltpu.SemaphoreType.DMA,
+            pltpu.SemaphoreType.DMA((tokens // block,)),
+            pltpu.SemaphoreType.DMA((tokens // block,)),
+        ],
+        compiler_params=params(24),
+        cost_estimate=cost(6 * 10**8, 12 * 10**6),
+    )(far(coupled), far(value), far(gate_values), entering, run, spread)
+    squares = lax.all_to_all(squares, "mp", 0, 0, tiled=True)
+
+    slots = min(4, tokens // block)
+    return pl.pallas_call(
+        functools.partial(normal_kernel, float(channels * groups)),
+        in_specs=[near_spec] * 3,
+        out_specs=any_spec,
+        out_shape=jax.ShapeDtypeStruct((tokens, channels), BF16),
+        scratch_shapes=[
+            pltpu.VMEM((chunks, CHUNK), F32),
+            pltpu.VMEM((slots, block, channels), BF16),
+            pltpu.SemaphoreType.DMA((slots,)),
         ],
         compiler_params=params(16),
-        cost_estimate=cost(6 * 10**8, 12 * 10**6),
-    )(
-        far(coupled), entering, far(value), far(gate_values), run, far(spread), far(norm_gain[None, :])
-    )
-    squares = lax.all_to_all(squares, "mp", 0, 0, tiled=True)
-
-    return pl.pallas_call(
-        functools.partial(normal_kernel, float(channels * groups)),
-        grid=(tokens // block,),
-        in_specs=[
-            pl.BlockSpec((block, channels), lambda i: (i, 0)),
-            whole((groups, chunks, CHUNK)),
-        ],
-        out_specs=pl.BlockSpec((block, channels), lambda i: (i, 0)),
-        out_shape=jax.ShapeDtypeStruct((tokens, channels), BF16),
-        scratch_shapes=[pltpu.VMEM((chunks, CHUNK, LANES), F32)],
-        compiler_params=params(16),
         cost_estimate=cost(10**7, 8 * 10**6),
-    )(gated, squares)
+    )(gated, squares, norm_gain[None, :])
 
 
 def solution(mesh):

time: 83 us -> 80.9 us (0.975)
  Pallas kernels: 42.8 us -> 41 us
    pallas_call x1, Pallas kernels: 4.36 us -> 2.48 us  [on_device(): pl.pallas_call(functools.partial(normal_kernel, float(channels * groups))...]
  transfers between devices with their start and end apart: 3 -> 3, of which waited for: 2 -> 2; matrix products, arithmetic and copies ran while one was open for 0% -> 0% of each run, Pallas kernels for 18% -> 19%
where the time goes in v4:
time: 80.9 us; the launch traced here: 80 us
  Pallas kernels  41 us (51%)
  blocking collectives  19.7 us (24%)
  starting transfers between devices  14.8 us (18%)
  waiting for transfers between devices  4.55 us (6%)
    all_to_all x1, blocking collectives, on_device(): squares = lax.all_to_all(squares, 'mp', 0, 0, tiled=True)  19.7 us
    pallas_call x2, Pallas kernels, inside(): pl.pallas_call(inside_kernel, grid=(count,), in_specs=[pl.BlockSpec((bloc...  13.8 us
    pallas_call x1, Pallas kernels, on_device(): pl.pallas_call(ends_kernel, grid=(tokens // block,), in_specs=[pl.BlockSp...  12.9 us
    pallas_call x1, Pallas kernels, on_device(): pl.pallas_call(gated_kernel, in_specs=[any_spec] * 3 + [near_spec] * 3, o...  8.63 us
    all_to_all x1, starting transfers between devices, on_device(): gathered = lax.all_to_all(ends, 'seq', 0, 0, tiled=True)  6.55 us
    all_to_all x1, starting transfers between devices, on_device(): lax.all_to_all(starts, 'seq', 0, 0, tiled=True).reshape(LANES, channels)  4.22 us
    ppermute x1, starting transfers between devices, on_device(): halo = lax.ppermute(tail, 'seq', [(i, i + 1) for i in range(sections - 1)])  4.01 us
    pallas_call x1, Pallas kernels, on_device(): pl.pallas_call(functools.partial(normal_kernel, float(channels * groups))...  2.48 us
  transfers between devices with their start and end apart: 3, of which 2 were waited for; matrix products, arithmetic and copies ran while one was open for 0% of the time, Pallas kernels for 19%

profile of v4, /device:TPU:1, one launch (start us, length us, event | category | flops | bytes accessed | tf_op | source)
XLA Modules:
  0.0 80.0 jit_solution(1021580357114645243)
XLA Ops:
  0.0 0.0 copy-start.2
  0.0 0.7 shard_map.109
  0.7 4.0 %collective-permute-start = (bf16[8,1280]{1,0:T(8,128)(2,1)S(1)}, bf16[8,1280]{1,0:T(8,128)(2,1)S(1)}, u32[]{:S(2)}, u32[]{:S(2)}) collective-permute-start(bf16[8,1280]{1,0:T(8,128)(2,1)S(1)} %shard_map.109), channel_id=1, source_target_pairs={{0,16},{16,32},{32,48},{48,64},{64,80},{80,96},{96,112},{112,128},... | collective-permute-start | bytes 61448 | tf_op jit(solution)/shard_map/ppermute | solution.py:365
  4.8 0.0 copy-done.2
  4.8 1.5 %shard_map.110 = (f32[16,32,128]{2,1,0:T(8,128)S(1)}, bf16[16,32,128]{2,1,0:T(8,128)(2,1)S(1)}, bf16[16,32,128]{2,1,0:T(8,128)(2,1)S(1)}, bf16[16,32,128]{2,1,0:T(8,128)(2,1)S(1)}, bf16[32,128]{1,0:T(8,128)(2,1)S(1)}) custom-call(f32[16,2048]{1,0:T(8,128)} %raw_ref.1, f32[1,16]{1,0:T(1,128)S(1)} %bitcast.7), custom_call_target="tpu_custom_call" | custom-call | flops 10000000 | bytes 1000000 | tf_op jit(solution)/shard_map/pallas_call | solution.py:370
  6.3 0.0 collective-permute-done.halo_ref
  6.3 12.9 %shard_map.111 = (bf16[2048,1024]{1,0:T(8,128)(2,1)}, bf16[2048,256]{1,0:T(8,128)(2,1)}, bf16[16,128,1024]{2,1,0:T(8,128)(2,1)}, bf16[16,16,1024]{2,1,0:T(8,128)(2,1)}) custom-call(bf16[2048,1024]{1,0:T(8,128)(2,1)} %feat_ref.3, bf16[2048,256]{1,0:T(8,128)(2,1)} %coup_ref.3, bf16[8,1280]{1,0:T(8,128)(2,1)S(1)} %collective-permute-done.halo_ref, ...), custom_call_target="tpu_custom_call" | custom-call | flops 1000000000 | bytes 10000000 | tf_op jit(solution)/shard_map/pallas_call | solution.py:392
  19.2 6.5 %all-to-all-start = ((bf16[16,16,1024]{2,1,0:T(8,128)(2,1)}), bf16[16,16,1024]{2,1,0:T(8,128)(2,1)S(1)}, u32[]{:S(2)}, u32[]{:S(2)}) async-start(bf16[16,16,1024]{2,1,0:T(8,128)(2,1)} %get-tuple-element.23), calls=%async_computation | async-start | bytes 1048576 | tf_op jit(solution)/shard_map/all_to_all | solution.py:462
  25.7 6.8 %shard_map.112.order_ref.rest_0_ = bf16[2048,1024]{1,0:T(8,128)(2,1)} custom-call(bf16[2048,1024]{1,0:T(8,128)(2,1)} %get-tuple-element.19.filt_ref, bf16[2048,256]{1,0:T(8,128)(2,1)} %get-tuple-element.18.coupled_ref, f32[16,32,128]{2,1,0:T(8,128)S(1)} %get-tuple-element.20.row_ref, bf16[16,32,128]{2,1,0:T(8,128)(2,1)S(1)} %get-tuple-element.21.ex_ref, ...), custom_call_target="tpu_custom_call" | custom-call | flops 2400000000 | bytes 8000000 | tf_op jit(solution)/shard_map/pallas_call | solution.py:440
  32.5 2.4 %all-to-all-done.pay_ref = bf16[16,16,1024]{2,1,0:T(8,128)(2,1)S(1)} async-done(((bf16[16,16,1024]{2,1,0:T(8,128)(2,1)}), bf16[16,16,1024]{2,1,0:T(8,128)(2,1)S(1)}, u32[]{:S(2)}, u32[]{:S(2)}) %all-to-all-start) | async-done | bytes 524320 | tf_op jit(solution)/shard_map/all_to_all | solution.py:462
  34.9 0.9 %shard_map.113.order_ref = f32[16,8,1024]{2,1,0:T(8,128)} custom-call(bf16[16,16,1024]{2,1,0:T(8,128)(2,1)S(1)} %all-to-all-done.pay_ref, bf16[2048,1024]{1,0:T(8,128)(2,1)} %shard_map.112.order_ref.rest_0_), custom_call_target="tpu_custom_call" | custom-call | flops 1000000 | bytes 1000000 | tf_op jit(solution)/shard_map/pallas_call | solution.py:464
  35.9 4.2 %all-to-all-start.1 = ((f32[16,8,1024]{2,1,0:T(8,128)}), f32[16,8,1024]{2,1,0:T(8,128)S(1)}, u32[]{:S(2)}, u32[]{:S(2)}) async-start(f32[16,8,1024]{2,1,0:T(8,128)} %shard_map.113.order_ref), calls=%async_computation.1 | async-start | bytes 1048576 | tf_op jit(solution)/shard_map/all_to_all | solution.py:473
  40.1 0.0 copy-start
  40.1 7.0 %shard_map.114.value_ref = bf16[2048,1024]{1,0:T(8,128)(2,1)} custom-call(bf16[2048,1024]{1,0:T(8,128)(2,1)} %get-tuple-element.19.filt_ref, bf16[2048,256]{1,0:T(8,128)(2,1)} %get-tuple-element.18.coupled_ref, f32[16,32,128]{2,1,0:T(8,128)S(1)} %get-tuple-element.20.row_ref, ...), custom_call_target="tpu_custom_call", output_to_operand_aliasing={{}: (7, {})} | custom-call | flops 2400000000 | bytes 8000000 | tf_op jit(solution)/shard_map/pallas_call | solution.py:440
  47.1 2.1 %all-to-all-done.1 = f32[16,8,1024]{2,1,0:T(8,128)S(1)} async-done(((f32[16,8,1024]{2,1,0:T(8,128)}), f32[16,8,1024]{2,1,0:T(8,128)S(1)}, u32[]{:S(2)}, u32[]{:S(2)}) %all-to-all-start.1) | async-done | bytes 524320 | tf_op jit(solution)/shard_map/all_to_all | solution.py:473
  49.3 0.0 copy-done
  49.3 0.0 copy-start.1
  49.3 8.6 %shard_map.115 = (bf16[2048,1024]{1,0:T(8,128)(2,1)S(1)}, bf16[16,16,128]{2,1,0:T(8,128)(2,1)S(1)}) custom-call(bf16[2048,256]{1,0:T(8,128)(2,1)} %get-tuple-element.18.coupled_ref, bf16[2048,1024]{1,0:T(8,128)(2,1)} %shard_map.114.value_ref, bf16[2048,1024]{1,0:T(8,128)(2,1)} %gate_ref.1, f32[128,1024]{1,0:T(8,128)S(1)} %bitcast.5, ...), custom_call_target="tpu_custom_call" | custom-call | flops 600000000 | bytes 12000000 | tf_op jit(solution)/shard_map/pallas_call | solution.py:476
  57.9 19.7 %all_to_all.15.sums_ref = bf16[16,16,128]{2,1,0:T(8,128)(2,1)S(1)} all-to-all(bf16[16,16,128]{2,1,0:T(8,128)(2,1)S(1)} %get-tuple-element.26), channel_id=1, replica_groups=mesh['seq'=16,'mp'=16] {'mp'}, dimensions={0} | all-to-all | bytes 131072 | tf_op jit(solution)/shard_map/all_to_all | solution.py:497
  77.6 0.0 copy-done.1
  77.6 2.5 %shard_map.116 = bf16[2048,1024]{1,0:T(8,128)(2,1)} custom-call(bf16[2048,1024]{1,0:T(8,128)(2,1)S(1)} %get-tuple-element.25.gated_ref, bf16[16,16,128]{2,1,0:T(8,128)(2,1)S(1)} %all_to_all.15.sums_ref, f32[1,1024]{1,0:T(1,128)S(1)} %bitcast.6), custom_call_target="tpu_custom_call" | custom-call | flops 10000000 | bytes 8000000 | tf_op jit(solution)/shard_map/pallas_call | solution.py:500
Async XLA Ops:
  0.0 4.8 %copy-start.2 = (f32[16]{0:T(128)S(1)}, f32[16]{0:T(128)}, u32[]{:S(2)}) copy-start(f32[16]{0:T(128)} %param.15) | copy-start | bytes 196
  0.7 5.5 %collective-permute-start = (bf16[8,1280]{1,0:T(8,128)(2,1)S(1)}, bf16[8,1280]{1,0:T(8,128)(2,1)S(1)}, u32[]{:S(2)}, u32[]{:S(2)}) collective-permute-start(bf16[8,1280]{1,0:T(8,128)(2,1)S(1)} %shard_map.109), channel_id=1, source_target_pairs={{0,16},{16,32},{32,48},{48,64},{64,80},{80,96},{96,112},{112,128},... | collective-permute-start | bytes 61448 | tf_op jit(solution)/shard_map/ppermute | solution.py:365
  19.2 15.7 %all-to-all-start = ((bf16[16,16,1024]{2,1,0:T(8,128)(2,1)}), bf16[16,16,1024]{2,1,0:T(8,128)(2,1)S(1)}, u32[]{:S(2)}, u32[]{:S(2)}) async-start(bf16[16,16,1024]{2,1,0:T(8,128)(2,1)} %get-tuple-element.23), calls=%async_computation | async-start | bytes 1048576 | tf_op jit(solution)/shard_map/all_to_all | solution.py:462
  35.9 13.4 %all-to-all-start.1 = ((f32[16,8,1024]{2,1,0:T(8,128)}), f32[16,8,1024]{2,1,0:T(8,128)S(1)}, u32[]{:S(2)}, u32[]{:S(2)}) async-start(f32[16,8,1024]{2,1,0:T(8,128)} %shard_map.113.order_ref), calls=%async_computation.1 | async-start | bytes 1048576 | tf_op jit(solution)/shard_map/all_to_all | solution.py:473
  40.1 9.1 %copy-start = (bf16[32,1024]{1,0:T(8,128)(2,1)S(1)}, bf16[32,1024]{1,0:T(8,128)(2,1)}, u32[]{:S(2)}) copy-start(bf16[32,1024]{1,0:T(8,128)(2,1)} %constant.2.clone.spread_ref) | copy-start | bytes 196612
  49.3 28.3 %copy-start.1 = (f32[1024]{0:T(1024)S(1)}, f32[1024]{0:T(1024)}, u32[]{:S(2)}) copy-start(f32[1024]{0:T(1024)} %param.20) | copy-start | bytes 12292

commit v5 on v4

--- a/solution.py
+++ b/solution.py
@@ -348,6 +348,7 @@
     chunks = tokens // CHUNK
     share = LANES // sections
     any_spec = pl.BlockSpec(memory_space=pl.ANY)
+    near_spec = pl.BlockSpec(memory_space=pltpu.VMEM)
 
     block = 2 * CHUNK
     tail = pl.pallas_call(
@@ -369,15 +370,8 @@
 
     rows, wch, ex, run, table = pl.pallas_call(
         decay_kernel,
-        grid=(1,),
-        in_specs=[whole((heads, tokens)), whole((1, heads))],
-        out_specs=(
-            whole((chunks, 2 * heads, CHUNK)),
-            whole((chunks, 2 * heads, CHUNK)),
-            whole((chunks, 2 * heads, CHUNK)),
-            whole((chunks, 2 * heads, CHUNK)),
-            whole((2 * heads, LANES)),
-        ),
+        in_specs=[near_spec] * 2,
+        out_specs=(near_spec,) * 5,
         out_shape=(
             pltpu.VMEM((chunks, 2 * heads, CHUNK), F32),
             pltpu.VMEM((chunks, 2 * heads, CHUNK), BF16),
@@ -387,7 +381,7 @@
         ),
         compiler_params=params(8),
         cost_estimate=cost(10**7, 10**6, 10**5),
-    )(far(step_raw), decay_log[None, :])
+    )(step_raw, decay_log[None, :])
 
     filtered, coupled, states, ends = pl.pallas_call(
         ends_kernel,
@@ -463,16 +457,14 @@
     value = inside(0, half, table)
     starts = pl.pallas_call(
         relay_kernel,
-        grid=(1,),
-        in_specs=[whole((sections, share + 8, channels)), any_spec],
-        out_specs=whole((sections, share, channels)),
+        in_specs=[near_spec, any_spec],
+        out_specs=near_spec,
         out_shape=jax.ShapeDtypeStruct((sections, share, channels), F32),
         compiler_params=params(8),
         cost_estimate=cost(10**6, 10**6),
     )(gathered, far(value))
     entering = lax.all_to_all(starts, "seq", 0, 0, tiled=True).reshape(LANES, channels)
     value = inside(half, steps - half, starts, far(value))
-    near_spec = pl.BlockSpec(memory_space=pltpu.VMEM)
     gated, squares = pl.pallas_call(
         gated_kernel,
         in_specs=[any_spec] * 3 + [near_spec] * 3,

time: 80.9 us -> 80.8 us (level)
  Pallas kernels: 41 us -> 40 us
    pallas_call x2, Pallas kernels: 2.44 us -> 1.54 us  [the longest x1 0.95 us: on_device(): pl.pallas_call(relay_kernel, in_specs=[near_spec, any_spec], out_specs=ne...]
  transfers between devices with their start and end apart: 3 -> 3, of which waited for: 2 -> 3; matrix products, arithmetic and copies ran while one was open for 0% -> 0% of each run, Pallas kernels for 19% -> 18%
where the time goes in v5:
time: 80.8 us; the launch traced here: 80.1 us
  Pallas kernels  40 us (50%)
  blocking collectives  19.7 us (24%)
  starting transfers between devices  15.4 us (19%)
  waiting for transfers between devices  4.87 us (6%)
    all_to_all x1, blocking collectives, on_device(): squares = lax.all_to_all(squares, 'mp', 0, 0, tiled=True)  19.7 us
    pallas_call x2, Pallas kernels, inside(): pl.pallas_call(inside_kernel, grid=(count,), in_specs=[pl.BlockSpec((bloc...  13.7 us
    pallas_call x1, Pallas kernels, on_device(): pl.pallas_call(ends_kernel, grid=(tokens // block,), in_specs=[pl.BlockSp...  12.9 us
    pallas_call x1, Pallas kernels, on_device(): pl.pallas_call(gated_kernel, in_specs=[any_spec] * 3 + [near_spec] * 3, o...  8.62 us
    all_to_all x1, starting transfers between devices, on_device(): gathered = lax.all_to_all(ends, 'seq', 0, 0, tiled=True)  7.19 us
    all_to_all x1, starting transfers between devices, on_device(): lax.all_to_all(starts, 'seq', 0, 0, tiled=True).reshape(LANES, channels)  4.2 us
    ppermute x1, starting transfers between devices, on_device(): halo = lax.ppermute(tail, 'seq', [(i, i + 1) for i in range(sections - 1)])  4.01 us
    pallas_call x1, Pallas kernels, on_device(): pl.pallas_call(functools.partial(normal_kernel, float(channels * groups))...  2.48 us
  transfers between devices with their start and end apart: 3, of which 3 were waited for; matrix products, arithmetic and copies ran while one was open for 0% of the time, Pallas kernels for 18%

profile of v5, /device:TPU:1, one launch (start us, length us, event | category | flops | bytes accessed | tf_op | source)
XLA Modules:
  0.0 80.1 jit_solution(3462122591581724034)
XLA Ops:
  0.0 0.0 copy-start.3
  0.0 0.0 copy-start.2
  0.0 0.8 shard_map.109
  0.8 4.0 %collective-permute-start = (bf16[8,1280]{1,0:T(8,128)(2,1)S(1)}, bf16[8,1280]{1,0:T(8,128)(2,1)S(1)}, u32[]{:S(2)}, u32[]{:S(2)}) collective-permute-start(bf16[8,1280]{1,0:T(8,128)(2,1)S(1)} %shard_map.109), channel_id=1, source_target_pairs={{0,16},{16,32},{32,48},{48,64},{64,80},{80,96},{96,112},{112,128},... | collective-permute-start | bytes 61448 | tf_op jit(solution)/shard_map/ppermute | solution.py:366
  4.8 0.0 copy-done.3
  4.8 0.0 copy-done.2
  4.8 0.6 shard_map.110
  5.4 0.3 collective-permute-done.halo_ref
  5.7 12.9 %shard_map.111 = (bf16[2048,1024]{1,0:T(8,128)(2,1)}, bf16[2048,256]{1,0:T(8,128)(2,1)}, bf16[16,128,1024]{2,1,0:T(8,128)(2,1)}, bf16[16,16,1024]{2,1,0:T(8,128)(2,1)}) custom-call(bf16[2048,1024]{1,0:T(8,128)(2,1)} %feat_ref.3, bf16[2048,256]{1,0:T(8,128)(2,1)} %coup_ref.3, bf16[8,1280]{1,0:T(8,128)(2,1)S(1)} %collective-permute-done.halo_ref, ...), custom_call_target="tpu_custom_call" | custom-call | flops 1000000000 | bytes 10000000 | tf_op jit(solution)/shard_map/pallas_call | solution.py:386
  18.6 7.2 %all-to-all-start = ((bf16[16,16,1024]{2,1,0:T(8,128)(2,1)}), bf16[16,16,1024]{2,1,0:T(8,128)(2,1)S(1)}, u32[]{:S(2)}, u32[]{:S(2)}) async-start(bf16[16,16,1024]{2,1,0:T(8,128)(2,1)} %get-tuple-element.23), calls=%async_computation | async-start | bytes 1048576 | tf_op jit(solution)/shard_map/all_to_all | solution.py:456
  25.8 6.7 %shard_map.112.order_ref.rest_0_ = bf16[2048,1024]{1,0:T(8,128)(2,1)} custom-call(bf16[2048,1024]{1,0:T(8,128)(2,1)} %get-tuple-element.19.filt_ref, bf16[2048,256]{1,0:T(8,128)(2,1)} %get-tuple-element.18.coupled_ref, f32[16,32,128]{2,1,0:T(8,128)S(1)} %get-tuple-element.20.row_ref, bf16[16,32,128]{2,1,0:T(8,128)(2,1)S(1)} %get-tuple-element.21.ex_ref, ...), custom_call_target="tpu_custom_call" | custom-call | flops 2400000000 | bytes 8000000 | tf_op jit(solution)/shard_map/pallas_call | solution.py:434
  32.5 2.4 %all-to-all-done.pay_ref = bf16[16,16,1024]{2,1,0:T(8,128)(2,1)S(1)} async-done(((bf16[16,16,1024]{2,1,0:T(8,128)(2,1)}), bf16[16,16,1024]{2,1,0:T(8,128)(2,1)S(1)}, u32[]{:S(2)}, u32[]{:S(2)}) %all-to-all-start) | async-done | bytes 524320 | tf_op jit(solution)/shard_map/all_to_all | solution.py:456
  35.0 1.0 %shard_map.113.order_ref = f32[16,8,1024]{2,1,0:T(8,128)} custom-call(bf16[16,16,1024]{2,1,0:T(8,128)(2,1)S(1)} %all-to-all-done.pay_ref, bf16[2048,1024]{1,0:T(8,128)(2,1)} %shard_map.112.order_ref.rest_0_), custom_call_target="tpu_custom_call" | custom-call | flops 1000000 | bytes 1000000 | tf_op jit(solution)/shard_map/pallas_call | solution.py:458
  35.9 4.2 %all-to-all-start.1 = ((f32[16,8,1024]{2,1,0:T(8,128)}), f32[16,8,1024]{2,1,0:T(8,128)S(1)}, u32[]{:S(2)}, u32[]{:S(2)}) async-start(f32[16,8,1024]{2,1,0:T(8,128)} %shard_map.113.order_ref), calls=%async_computation.1 | async-start | bytes 1048576 | tf_op jit(solution)/shard_map/all_to_all | solution.py:466
  40.1 0.0 copy-start
  40.2 7.0 %shard_map.114.value_ref = bf16[2048,1024]{1,0:T(8,128)(2,1)} custom-call(bf16[2048,1024]{1,0:T(8,128)(2,1)} %get-tuple-element.19.filt_ref, bf16[2048,256]{1,0:T(8,128)(2,1)} %get-tuple-element.18.coupled_ref, f32[16,32,128]{2,1,0:T(8,128)S(1)} %get-tuple-element.20.row_ref, ...), custom_call_target="tpu_custom_call", output_to_operand_aliasing={{}: (7, {})} | custom-call | flops 2400000000 | bytes 8000000 | tf_op jit(solution)/shard_map/pallas_call | solution.py:434
  47.1 2.1 %all-to-all-done.1 = f32[16,8,1024]{2,1,0:T(8,128)S(1)} async-done(((f32[16,8,1024]{2,1,0:T(8,128)}), f32[16,8,1024]{2,1,0:T(8,128)S(1)}, u32[]{:S(2)}, u32[]{:S(2)}) %all-to-all-start.1) | async-done | bytes 524320 | tf_op jit(solution)/shard_map/all_to_all | solution.py:466
  49.3 0.0 copy-done
  49.3 0.0 copy-start.1
  49.3 8.6 %shard_map.115 = (bf16[2048,1024]{1,0:T(8,128)(2,1)S(1)}, bf16[16,16,128]{2,1,0:T(8,128)(2,1)S(1)}) custom-call(bf16[2048,256]{1,0:T(8,128)(2,1)} %get-tuple-element.18.coupled_ref, bf16[2048,1024]{1,0:T(8,128)(2,1)} %shard_map.114.value_ref, bf16[2048,1024]{1,0:T(8,128)(2,1)} %gate_ref.1, f32[128,1024]{1,0:T(8,128)S(1)} %bitcast.5, ...), custom_call_target="tpu_custom_call" | custom-call | flops 600000000 | bytes 12000000 | tf_op jit(solution)/shard_map/pallas_call | solution.py:468
  57.9 19.7 %all_to_all.15.sums_ref = bf16[16,16,128]{2,1,0:T(8,128)(2,1)S(1)} all-to-all(bf16[16,16,128]{2,1,0:T(8,128)(2,1)S(1)} %get-tuple-element.26), channel_id=1, replica_groups=mesh['seq'=16,'mp'=16] {'mp'}, dimensions={0} | all-to-all | bytes 131072 | tf_op jit(solution)/shard_map/all_to_all | solution.py:489
  77.6 0.0 copy-done.1
  77.6 2.5 %shard_map.116 = bf16[2048,1024]{1,0:T(8,128)(2,1)} custom-call(bf16[2048,1024]{1,0:T(8,128)(2,1)S(1)} %get-tuple-element.25.gated_ref, bf16[16,16,128]{2,1,0:T(8,128)(2,1)S(1)} %all_to_all.15.sums_ref, f32[1,1024]{1,0:T(1,128)S(1)} %bitcast.6), custom_call_target="tpu_custom_call" | custom-call | flops 10000000 | bytes 8000000 | tf_op jit(solution)/shard_map/pallas_call | solution.py:492
Async XLA Ops:
  0.0 4.8 %copy-start.3 = (f32[16]{0:T(128)S(1)}, f32[16]{0:T(128)}, u32[]{:S(2)}) copy-start(f32[16]{0:T(128)} %param.15) | copy-start | bytes 196
  0.0 4.8 %copy-start.2 = (f32[16,2048]{1,0:T(8,128)S(1)}, f32[16,2048]{1,0:T(8,128)}, u32[]{:S(2)}) copy-start(f32[16,2048]{1,0:T(8,128)} %raw_ref.1) | copy-start | bytes 393220
  0.8 4.9 %collective-permute-start = (bf16[8,1280]{1,0:T(8,128)(2,1)S(1)}, bf16[8,1280]{1,0:T(8,128)(2,1)S(1)}, u32[]{:S(2)}, u32[]{:S(2)}) collective-permute-start(bf16[8,1280]{1,0:T(8,128)(2,1)S(1)} %shard_map.109), channel_id=1, source_target_pairs={{0,16},{16,32},{32,48},{48,64},{64,80},{80,96},{96,112},{112,128},... | collective-permute-start | bytes 61448 | tf_op jit(solution)/shard_map/ppermute | solution.py:366
  18.6 16.4 %all-to-all-start = ((bf16[16,16,1024]{2,1,0:T(8,128)(2,1)}), bf16[16,16,1024]{2,1,0:T(8,128)(2,1)S(1)}, u32[]{:S(2)}, u32[]{:S(2)}) async-start(bf16[16,16,1024]{2,1,0:T(8,128)(2,1)} %get-tuple-element.23), calls=%async_computation | async-start | bytes 1048576 | tf_op jit(solution)/shard_map/all_to_all | solution.py:456
  35.9 13.4 %all-to-all-start.1 = ((f32[16,8,1024]{2,1,0:T(8,128)}), f32[16,8,1024]{2,1,0:T(8,128)S(1)}, u32[]{:S(2)}, u32[]{:S(2)}) async-start(f32[16,8,1024]{2,1,0:T(8,128)} %shard_map.113.order_ref), calls=%async_computation.1 | async-start | bytes 1048576 | tf_op jit(solution)/shard_map/all_to_all | solution.py:466
  40.1 9.1 %copy-start = (bf16[32,1024]{1,0:T(8,128)(2,1)S(1)}, bf16[32,1024]{1,0:T(8,128)(2,1)}, u32[]{:S(2)}) copy-start(bf16[32,1024]{1,0:T(8,128)(2,1)} %constant.2.clone.spread_ref) | copy-start | bytes 196612
  49.3 28.3 %copy-start.1 = (f32[1024]{0:T(1024)S(1)}, f32[1024]{0:T(1024)}, u32[]{:S(2)}) copy-start(f32[1024]{0:T(1024)} %param.20) | copy-start | bytes 12292
